TPU v7x, 32 devices: a whole 2x2x4 slice. The times are simulated.
32 devices in a mesh: dev: 32 (over z, y, x, core).
Axes of the slice: x: 2, y: 2, z: 4, core: 2. Of those that a mesh axis runs over, the one named last changes fastest.
Arguments:
- state: float32 [5, 64, 16384], P(None, None, 'dev'), as said below
- step_size: float32 [1], replicated, may hold values from 0.0003 to 0.0006
- levels: int32 [16384], P('dev'), may hold values from 6 to 7, as said below
- send_faces: int32 [256, 128], P('dev'), may hold values from 0 to 3072, as said below
- partner: int32 [6, 16384], P(None, 'dev'), may hold values from 0 to 4096, as said below
- mortar_in: int32 [5, 1280], P(None, 'dev'), may hold values from 0 to 4096, as said below
- mortar_dir: int32 [1280], P('dev'), may hold values from 0 to 3, as said below
- return_faces: int32 [64, 32], P('dev'), may hold values from 0 to 200, as said below
- flux_source: int32 [6, 16384], P(None, 'dev'), may hold values from 0 to 264, as said below
Outputs:
- increment: float32 [5, 64, 16384], P(None, None, 'dev')
Inputs may be any that keep to these rules, and one draw needn't show every extreme that they name: At every node the entries are density, momenta and total energy of a state with density from 1 to 1.5, velocity components from -0.2 to 0.2 and pressure from 1 to 1.5. `levels`: every element has level 6 or 7. `send_faces`: row 8 d + p lists local face numbers of device d whose traces its peer p needs; 3072 marks an empty entry. Faces are either conforming (opposite faces of two elements of one level, each the other's partner) or hanging (one face and four faces of elements one level finer meet in exactly one mortar); partners lie within 4 devices along the curve, mortars join faces of one device or of two adjacent ones. Hanging faces have partner 6 * 512. `mortar_in`: unused mortar entries name 3072 in all five rows. `mortar_dir`: unused mortar entries have 0. `return_faces`: 200 marks an empty entry. `flux_source`: 200 exactly for conforming faces.
All inputs are finite; a program needn't handle non-finite values.
Results may differ from a plain program's by a relative error of at most 0.0003.
Values sent between devices are 32-bit elements; how exact they have to be, the bound alone decides.
No kernel may reach another device: no remote copies, remote signals or barrier semaphores. Data moves between devices by JAX's collectives and lax.ppermute only.
A program may use at most 64 MiB of HBM per device.

v0:
```python
import functools

import jax
import jax.numpy as jnp
import numpy as np
from jax import lax
from jax.experimental import pallas as pl
from jax.experimental.pallas import tpu as pltpu
from jax.sharding import PartitionSpec as P


GAMMA = 1.4
HIGHEST = lax.Precision.HIGHEST
F32 = jnp.float32
BF16 = jnp.bfloat16
LANES = 128


def passed_along(block, axis, distance):
    devices = range(lax.axis_size(axis))
    route = [((i - distance) % len(devices), i) for i in devices]
    return lax.ppermute(block, axis, route)


def lobatto_tables():
    nodes = np.array([-1.0, -1.0 / np.sqrt(5.0), 1.0 / np.sqrt(5.0), 1.0])
    weights = np.array([1.0, 5.0, 5.0, 1.0]) / 6.0

    def basis(points):
        table = np.ones((len(points), 4))
        for column in range(4):
            for other in range(4):
                if other != column:
                    table[:, column] *= (points - nodes[other]) / (nodes[column] - nodes[other])
        return table

    derivative = np.zeros((4, 4))
    for row in range(4):
        for column in range(4):
            total = 0.0
            for other in range(4):
                if other != column:
                    term = 1.0 / (nodes[column] - nodes[other])
                    for third in range(4):
                        if third != column and third != other:
                            term *= (nodes[row] - nodes[third]) / (nodes[column] - nodes[third])
                    total += term
            derivative[row, column] = total
    lower = basis((nodes - 1.0) / 2.0)
    upper = basis((nodes + 1.0) / 2.0)
    back_lower = 0.5 * (lower.T * weights[None, :]) / weights[:, None]
    back_upper = 0.5 * (upper.T * weights[None, :]) / weights[:, None]
    return [
        np.asarray(table, np.float32)
        for table in (derivative, lower, upper, back_lower, back_upper)
    ]


def operator_tables():
    derivative, lower, upper, back_lower, back_upper = lobatto_tables()
    eye = np.eye(4, dtype=np.float32)
    volume = np.concatenate(
        [
            np.kron(derivative, np.kron(eye, eye)),
            np.kron(eye, np.kron(derivative, eye)),
            np.kron(eye, np.kron(eye, derivative)),
        ],
        axis=1,
    )
    five = np.eye(5, dtype=np.float32)
    forward, backward = (lower, upper), (back_lower, back_upper)
    spread = np.concatenate(
        [np.kron(five, np.kron(forward[q % 2], forward[q // 2])) for q in range(4)], axis=0
    )
    gather = np.concatenate(
        [np.kron(five, np.kron(backward[q % 2], backward[q // 2])) for q in range(4)], axis=1
    )
    return volume, spread, gather


def split_table(table):
    kind = jnp.dtype(BF16)
    high = table.astype(kind)
    rest = table - high.astype(np.float32)
    middle = rest.astype(kind)
    return high, middle, (rest - middle.astype(np.float32)).astype(kind)


def read_lanes(state_hbm, lanes, sems):
    return [
        pltpu.make_async_copy(
            state_hbm.at[:, :, pl.ds(block * LANES, LANES)], lanes.at[block], sems.at[block]
        )
        for block in range(lanes.shape[0])
    ]


def face_part(lanes, block, var, face):
    if face < 2:
        return lanes[block, var, 48 * face : 48 * face + 16, :]
    if face < 4:
        start = 12 * (face % 2)
        return jnp.concatenate(
            [lanes[block, var, 16 * i + start : 16 * i + start + 4, :] for i in range(4)], axis=0
        )
    return lanes[block, var, pl.ds(3 * (face % 2), 16, stride=4), :]


def add_face(lanes, var, face, value):
    for block in range(lanes.shape[0]):
        part = value[:, block * LANES : (block + 1) * LANES]
        if face < 2:
            lanes[block, var, 48 * face : 48 * face + 16, :] += part
        elif face < 4:
            start = 12 * (face % 2)
            for i in range(4):
                lanes[block, var, start + 16 * i : start + 16 * i + 4, :] += part[
                    4 * i : 4 * i + 4
                ]
        else:
            lanes[block, var, pl.ds(3 * (face % 2), 16, stride=4), :] += part


def three_pieces(value):
    high = value.astype(BF16)
    rest = value - high.astype(F32)
    middle = rest.astype(BF16)
    low = (rest - middle.astype(F32)).astype(BF16)
    return high, middle, low


def store_pieces(pieces, rows, columns, value):
    for which, piece in enumerate(three_pieces(value)):
        pieces[80 * which + rows : 80 * which + rows + value.shape[0], columns] = piece


ROWS = 512


def number_rows(grid):
    grid[...] = lax.broadcasted_iota(jnp.int32, grid.shape, 0).astype(jnp.int16)


def one_hot(grid, indices, count):
    width = indices.shape[1]
    rows = min(count, ROWS)
    row = jnp.broadcast_to(indices, (16, width)).astype(jnp.int16)
    spots = jnp.concatenate([grid[0:rows, :]] * (width // LANES), axis=1)
    parts = []
    for start in range(0, count, rows):
        want = jnp.concatenate([row - jnp.int16(start)] * (rows // 16), axis=0)
        parts.append(jnp.where(spots == want, jnp.ones((), BF16), jnp.zeros((), BF16)))
    return parts[0] if len(parts) == 1 else jnp.concatenate(parts, axis=0)


def joined(product):
    return (product[0:80] + product[80:160]) + product[160:240]


def primitives(cons):
    inverse = 1.0 / cons[0]
    motion = [cons[1 + axis] * inverse for axis in range(3)]
    pressure = (GAMMA - 1.0) * (
        cons[4] - 0.5 * (cons[1] * motion[0] + cons[2] * motion[1] + cons[3] * motion[2])
    )
    return inverse, motion, pressure


def axis_flux(cons, prim, axis, sign):
    _, motion, pressure = prim
    along = motion[axis] if sign > 0 else -motion[axis]
    push = pressure if sign > 0 else -pressure
    flux = [cons[v] * along for v in range(4)]
    flux[1 + axis] = flux[1 + axis] + push
    flux.append((cons[4] + pressure) * along)
    return flux


def sound(prim):
    inverse, _, pressure = prim
    return jnp.sqrt(GAMMA * pressure * inverse)


def normal_flux(cons, normal):
    inverse, motion, pressure = primitives(cons)
    along = motion[0] * normal[0] + motion[1] * normal[1] + motion[2] * normal[2]
    flux = [
        cons[0] * along,
        cons[1] * along + pressure * normal[0],
        cons[2] * along + pressure * normal[1],
        cons[3] * along + pressure * normal[2],
        (cons[4] + pressure) * along,
    ]
    return flux, jnp.abs(along) + jnp.sqrt(GAMMA * pressure * inverse)


def packed_places(count):
    return [0, count, 2 * count, LANES, LANES + count]


def highest(value):
    return jnp.max(value)


def send_kernel(hop, state_hbm, faces_ref, mortar_ref, way_ref, back_ref, *rest):
    peers, slots = faces_ref.shape
    outs = rest[:peers]
    lanes, traces, pieces, table, spots, grid, sems = rest[peers:]
    elems = state_hbm.shape[2]
    chunks = elems // LANES
    count, backs = mortar_ref.shape[1], back_ref.shape[1]
    copies = read_lanes(state_hbm, lanes, sems)
    for copy in copies:
        copy.start()

    wanted = [faces_ref[p : p + 1, :] for p in range(peers)]
    faces = faces_ref[...]
    face = sum((faces >= (k + 1) * elems).astype(jnp.int32) for k in range(6))
    least = jnp.min(jnp.where(face < 6, face, 5), axis=1, keepdims=True)
    most = jnp.max(jnp.where(face < 6, face, 0), axis=1, keepdims=True)
    longest = highest(most - least)
    starts = [least[p, 0] for p in range(peers)]
    stops = [most[p, 0] for p in range(peers)]

    number_rows(grid)
    table[...] = jnp.zeros(table.shape, F32)
    table[0:5, :] = mortar_ref[...].astype(F32)
    table[5:6, :] = way_ref[...].astype(F32)
    for side in range(2):
        for group in range(4):
            spots[side : side + 1, group * backs : (group + 1) * backs] = back_ref[
                side : side + 1, :
            ]
    lane = lax.broadcasted_iota(jnp.int32, (1, LANES), 1)
    group_of = sum((lane >= (k + 1) * backs).astype(jnp.int32) for k in range(3))
    empty = 6 * elems
    extra = []
    for side, target in ((0, 0), (1, hop)):
        entry = spots[side : side + 1, :]
        kind = sum((entry >= (k + 1) * count).astype(jnp.int32) for k in range(5))
        which = jnp.where(kind < 5, entry - kind * count, -1)
        rows = lax.broadcasted_iota(jnp.int32, (count, LANES), 0)
        found = jnp.dot(
            table[...],
            (rows == which).astype(F32),
            preferred_element_type=F32,
            precision=HIGHEST,
        )
        small = sum(jnp.where(group_of == k, found[1 + k : 2 + k], 0.0) for k in range(4))
        trace = jnp.where(kind == 0, small, found[0:1])
        unused = (kind == 5) | ((kind > 0) & (group_of > 0))
        trace = jnp.where(unused, float(empty), trace).astype(jnp.int32)
        slot = trace - (empty + 1) - (hop if side == 0 else 0) * slots
        code = jnp.where((trace > empty) & (slot >= 0) & (slot < slots), slot, -1)
        outs[target][80:88, slots:] = jnp.zeros((8, LANES), F32)
        outs[target][80:81, slots:] = code.astype(F32)
        outs[target][81:82, slots:] = kind.astype(F32)
        outs[target][82:83, slots:] = found[5:6]
        outs[target][80:88, 0:slots] = jnp.zeros((8, slots), F32)
        extra.append(trace)

    for copy in copies:
        copy.wait()
    for face in range(6):
        for var in range(5):
            for block in range(chunks):
                part = face_part(lanes, block, var, face)
                rows = slice(16 * var, 16 * var + 16)
                columns = slice(block * LANES, (block + 1) * LANES)
                traces[face, rows, columns] = part
                if face < 4:
                    store_pieces(
                        pieces,
                        16 * var,
                        slice(face * elems + block * LANES, face * elems + (block + 1) * LANES),
                        part,
                    )

    def collect(step, first):
        for p in range(peers):
            face = jnp.minimum(starts[p] + step, stops[p])
            local = wanted[p] - face * elems
            chunk_of = jnp.broadcast_to(lax.shift_right_arithmetic(local, 7), (8, LANES))
            spot = jnp.broadcast_to(jnp.bitwise_and(local, LANES - 1), (8, LANES))
            for r in range(10):
                rows = slice(8 * r, 8 * r + 8)
                value = jnp.zeros((8, LANES), F32) if first else outs[p][rows, 0:slots]
                for chunk in range(chunks):
                    part = traces[face, rows, chunk * LANES : (chunk + 1) * LANES]
                    value = jnp.where(
                        chunk_of == chunk, jnp.take_along_axis(part, spot, axis=1), value
                    )
                outs[p][rows, 0:slots] = value

    collect(0, True)
    product = jnp.dot(
        pieces[...],
        one_hot(grid, jnp.concatenate(extra, axis=1), 4 * elems),
        preferred_element_type=F32,
    )
    whole = joined(product)
    outs[0][0:80, slots:] = whole[:, 0:LANES]
    outs[hop][0:80, slots:] = whole[:, LANES:]

    @pl.loop(1, longest + 1)
    def _(step):
        collect(step, False)


def local_kernel(
    block_count,
    state_hbm,
    partner_ref,
    mortar_ref,
    source_ref,
    level_ref,
    step_ref,
    volume_ref,
    acc_ref,
    traces_ref,
    beside_ref,
    big_ref,
    own_ref,
    range_ref,
    lanes,
    pieces,
    spots,
    grid,
    sems,
):
    elems = state_hbm.shape[2]
    chunks = elems // LANES
    count = mortar_ref.shape[1]
    wide = 2 * LANES
    number_rows(grid)
    links = partner_ref[...]
    block = lax.shift_right_arithmetic(links - (6 * elems + 1), wide.bit_length() - 1)
    least = jnp.min(jnp.where(block >= 0, block, block_count), axis=1, keepdims=True)
    most = jnp.max(block, axis=1, keepdims=True)
    for face in range(6):
        range_ref[face] = jnp.minimum(least[face, 0], block_count - 1)
        range_ref[8 + face] = most[face, 0]
    range_ref[6] = highest(jnp.where(most > least, 1, 0))
    copies = read_lanes(state_hbm, lanes, sems)
    for copy in copies:
        copy.start()
    returned = own_ref.shape[1] // 2
    first_back = 5 * count + 1
    slot = lax.broadcasted_iota(jnp.int32, (returned, elems), 0) + first_back
    number = lax.broadcasted_iota(jnp.int32, (returned, elems), 1)
    hit = jnp.zeros((returned, elems), jnp.int32)
    for face in range(4):
        hit = jnp.where(source_ref[face : face + 1, :] == slot, number + (face * elems + 1), hit)
    column = jnp.sum(hit.astype(F32), axis=1, keepdims=True)
    corner = lax.broadcasted_iota(jnp.int32, (returned, LANES), 0) == lax.broadcasted_iota(
        jnp.int32, (returned, LANES), 1
    )
    owner = jnp.sum(jnp.where(corner, column, 0.0), axis=0, keepdims=True).astype(jnp.int32) - 1
    spots[...] = jnp.full(spots.shape, -1, jnp.int32)
    for row, place in enumerate(packed_places(count)):
        spots[0:1, place : place + count] = mortar_ref[row : row + 1, :]

    for copy in copies:
        copy.wait()
    for face in range(6):
        for var in range(5):
            rows = slice(16 * var, 16 * var + 16)
            for block in range(chunks):
                part = face_part(lanes, block, var, face)
                columns = slice(
                    face * elems + block * LANES, face * elems + (block + 1) * LANES
                )
                traces_ref[rows, columns] = part
                store_pieces(pieces, 16 * var, columns, part)
    for face in range(6):
        other = (face ^ 1) * elems
        product = jnp.dot(
            pieces[:, other : other + elems],
            one_hot(grid, partner_ref[face : face + 1, :] - other, elems),
            preferred_element_type=F32,
        )
        beside_ref[:, face * elems : (face + 1) * elems] = joined(product)
    wanted = spots[0:1, :]
    big_ref[...] = joined(
        jnp.dot(
            pieces[:, 0 : 4 * elems], one_hot(grid, wanted, 4 * elems), preferred_element_type=F32
        )
    )
    own_ref[...] = joined(
        jnp.dot(pieces[:, 0 : 4 * elems], one_hot(grid, owner, 4 * elems), preferred_element_type=F32)
    )
    factor = -step_ref[0] * jnp.left_shift(2, level_ref[...]).astype(F32)
    cons = [
        jnp.concatenate([lanes[block, v] for block in range(chunks)], axis=1) for v in range(5)
    ]
    prim = primitives(cons)
    fluxes = [axis_flux(cons, prim, axis, 1) for axis in range(3)]
    for var in range(5):
        stacked = jnp.concatenate([fluxes[axis][var] for axis in range(3)], axis=0)
        high, middle, low = three_pieces(stacked)
        first = jnp.dot(volume_ref[...], high, preferred_element_type=F32)
        second = jnp.dot(volume_ref[0:128, :], middle, preferred_element_type=F32)
        third = jnp.dot(volume_ref[0:64, :], low, preferred_element_type=F32)
        total = factor * (
            first[0:64]
            + ((first[64:128] + second[0:64]) + ((first[128:192] + second[64:128]) + third))
        )
        for block in range(chunks):
            acc_ref[block, var] = total[:, block * LANES : (block + 1) * LANES]


def with_reference(traces, empty):
    return jnp.concatenate(
        [
            jnp.where(empty, 1.0, traces[0:16]),
            jnp.where(empty, 0.0, traces[16:64]),
            jnp.where(empty, 2.5, traces[64:80]),
        ],
        axis=0,
    )


def mortar_stars(traces, way, spread, gather):
    normal = [
        (way == 2 * axis + 1).astype(F32) - (way == 2 * axis).astype(F32) for axis in range(3)
    ]
    near = jnp.dot(spread, traces[0], preferred_element_type=F32, precision=HIGHEST)
    stars = []
    for quarter in range(4):
        first = [near[80 * quarter + 16 * v : 80 * quarter + 16 * v + 16] for v in range(5)]
        second = [traces[1 + quarter][16 * v : 16 * v + 16] for v in range(5)]
        first_flux, first_speed = normal_flux(first, normal)
        second_flux, second_speed = normal_flux(second, normal)
        speed = jnp.maximum(first_speed, second_speed)
        stars.append(
            jnp.concatenate(
                [
                    0.5 * (first_flux[v] + second_flux[v]) - 0.5 * speed * (second[v] - first[v])
                    for v in range(5)
                ],
                axis=0,
            )
        )
    whole = jnp.dot(
        gather, jnp.concatenate(stars, axis=0), preferred_element_type=F32, precision=HIGHEST
    )
    return whole, stars


def finish_kernel(base, hop, peers, *rest):
    arrived = rest[:peers]
    (
        acc_ref,
        traces_ref,
        beside_ref,
        big_ref,
        own_ref,
        partner_ref,
        source_ref,
        faces_ref,
        mortar_ref,
        way_ref,
        level_ref,
        step_ref,
        spread_ref,
        gather_ref,
        range_ref,
        out_hbm,
        sums,
        outside,
        pieces,
        fluxes,
        stars_of,
        payload,
        spots,
        grid,
        sems,
    ) = rest[peers:]
    slots = faces_ref.shape[1]
    elems = partner_ref.shape[1]
    chunks = elems // LANES
    count = mortar_ref.shape[1]
    empty = base - 1
    wide = 2 * slots
    backs = LANES // 4
    places = packed_places(count)

    number_rows(grid)
    links = [partner_ref[face : face + 1, :] for face in range(6)]
    sources = [source_ref[face : face + 1, :] for face in range(4)]

    for peer in range(peers):
        for var in range(5):
            columns = slice((peer % 2) * slots, (peer % 2 + 1) * slots)
            for which, piece in enumerate(
                three_pieces(arrived[peer][16 * var : 16 * var + 16, 0:slots])
            ):
                row = 80 * which + 16 * var
                pieces[peer // 2, row : row + 16, columns] = piece
    payload[0] = arrived[0][:, slots:]
    payload[1] = arrived[hop][:, slots:]
    codes = [payload[side, 80:81, :] for side in range(2)]

    @pl.when(highest(jnp.maximum(codes[0], codes[1])) >= 0.0)
    def _():
        for side, row in ((0, hop), (1, 0)):
            code = codes[side].astype(jnp.int32)
            listed = jnp.take_along_axis(
                jnp.broadcast_to(faces_ref[row : row + 1, :], (8, LANES)),
                jnp.broadcast_to(jnp.maximum(code, 0), (8, LANES)),
                axis=1,
            )
            listed = jnp.where(jnp.broadcast_to(code, (8, LANES)) >= 0, listed, -1)
            chunk_of = lax.shift_right_arithmetic(listed, 7)
            spot = jnp.bitwise_and(listed, LANES - 1)
            for r in range(10):
                rows = slice(8 * r, 8 * r + 8)

                def pick(chunk, value):
                    start = pl.multiple_of(chunk * LANES, LANES)
                    part = traces_ref[rows, pl.ds(start, LANES)]
                    return jnp.where(
                        chunk_of == chunk, jnp.take_along_axis(part, spot, axis=1), value
                    )

                payload[side, rows, :] = lax.fori_loop(
                    0, 6 * chunks, pick, payload[side, rows, :]
                )

    @pl.when(range_ref[6] == 0)
    def _():
        outside[...] = jnp.zeros(outside.shape, F32)

    @pl.when(range_ref[6] != 0)
    def _():
        for face in range(6):
            outside[face] = jnp.zeros(outside.shape[1:], F32)

            @pl.loop(range_ref[face] + 1, range_ref[8 + face] + 1)
            def _(block, face=face):
                outside[face] += joined(
                    jnp.dot(
                        pieces[block],
                        one_hot(grid, links[face] - base - block * wide, wide),
                        preferred_element_type=F32,
                    )
                )

    factor = (-6.0 * step_ref[0]) * jnp.left_shift(2, level_ref[...]).astype(F32)
    sums[...] = acc_ref[...]
    for face in range(6):
        axis, sign = face // 2, 2 * (face % 2) - 1
        columns = slice(face * elems, (face + 1) * elems)
        block = range_ref[face]
        near = joined(
            jnp.dot(
                pieces[block],
                one_hot(grid, links[face] - base - block * wide, wide),
                preferred_element_type=F32,
            )
        )
        near = near + (beside_ref[:, columns] + outside[face])
        first = [traces_ref[16 * v : 16 * v + 16, columns] for v in range(5)]
        second = [near[16 * v : 16 * v + 16, :] for v in range(5)]
        first_prim, second_prim = primitives(first), primitives(second)
        first_flux = axis_flux(first, first_prim, axis, sign)
        second_flux = axis_flux(second, second_prim, axis, sign)
        speed = jnp.maximum(
            jnp.abs(first_prim[1][axis]) + sound(first_prim),
            jnp.abs(second_prim[1][axis]) + sound(second_prim),
        )
        hanging = links[face] == empty
        for v in range(5):
            star = 0.5 * (second_flux[v] - first_flux[v]) - 0.5 * speed * (second[v] - first[v])
            jump = jnp.where(hanging, -first_flux[v], star)
            if face < 4:
                stars_of[face, 16 * v : 16 * v + 16, :] = jump
            else:
                add_face(sums, v, face, factor * jump)

    spots[...] = jnp.full(spots.shape, empty, jnp.int32)
    for row, place in enumerate(places):
        spots[0:1, place : place + count] = mortar_ref[row : row + 1, :]
    spots[1:2, 0:count] = way_ref[...]
    packed = spots[0:1, :]
    total = jnp.zeros((240, wide), F32)
    for block in range(peers // 2):
        total = total + jnp.dot(
            pieces[block],
            one_hot(grid, packed - (base + block * wide), wide),
            preferred_element_type=F32,
        )
    both = with_reference(joined(total) + big_ref[...], packed == empty)
    local = []
    for row, place in enumerate(places):
        part = both[:, 0:LANES] if place < LANES else both[:, LANES:]
        shift = place % LANES
        local.append(part if shift == 0 else pltpu.roll(part, LANES - shift, 1))
    lane = lax.broadcasted_iota(jnp.int32, (1, LANES), 1)
    used = lane < count
    local = [with_reference(part, jnp.logical_not(used)) for part in local]
    local_way = jnp.where(used, spots[1:2, 0:LANES], 0)

    moved = []
    for group in range(4):
        shift = group * backs
        parts = [
            payload[0] if shift == 0 else pltpu.roll(payload[0], LANES - shift, 1),
            payload[1] if shift == backs else pltpu.roll(payload[1], (backs - shift) % LANES, 1),
        ]
        moved.append(jnp.where(lane < backs, parts[0], parts[1]))
    own = own_ref[...]
    unused = (lane >= 2 * backs) | (own[0:1] == 0.0)
    kind = jnp.where(unused, 0, moved[0][81:82].astype(jnp.int32))
    back_way = jnp.where(unused, 0, moved[0][82:83].astype(jnp.int32))
    large = kind == 0
    back = [jnp.where(large, own, moved[0][0:80])]
    for quarter in range(4):
        back.append(jnp.where(large, moved[quarter][0:80], own))
    back = [with_reference(part, unused) for part in back]

    traces = [jnp.concatenate([local[k], back[k]], axis=1) for k in range(5)]
    way = jnp.concatenate([local_way, back_way], axis=1)
    whole, stars = mortar_stars(traces, way, spread_ref[...], gather_ref[...])
    values = [whole[:, 0:LANES]] + [-star[:, 0:LANES] for star in stars]
    result = whole[:, LANES:]
    for quarter in range(4):
        result = jnp.where(kind == 1 + quarter, -stars[quarter][:, LANES:], result)
    halves = [jnp.zeros((80, LANES), F32), jnp.zeros((80, LANES), F32)]
    for row, place in enumerate(places):
        shift = place % LANES
        part = values[row] if shift == 0 else pltpu.roll(values[row], shift, 1)
        inside = (lane >= shift) & (lane < shift + count)
        halves[place // LANES] = jnp.where(inside, part, halves[place // LANES])
    for which, value in enumerate(halves + [result]):
        store_pieces(fluxes, 0, slice(which * LANES, (which + 1) * LANES), value[0:16])
        for var in range(1, 5):
            store_pieces(
                fluxes,
                16 * var,
                slice(which * LANES, (which + 1) * LANES),
                value[16 * var : 16 * var + 16],
            )

    for face in range(4):
        entry = sources[face]
        row = sum((entry >= (k + 1) * count).astype(jnp.int32) for k in range(4))
        spot = entry - row * count
        column = jnp.where(row >= 3, LANES + (row - 3) * count, row * count) + spot
        beyond = 2 * LANES + entry - (5 * count + 1)
        column = jnp.where(entry < 5 * count, column, jnp.where(entry > 5 * count, beyond, -1))
        star = joined(
            jnp.dot(
                fluxes[...], one_hot(grid, column, 3 * LANES), preferred_element_type=F32
            )
        )
        for v in range(5):
            rows = slice(16 * v, 16 * v + 16)
            add_face(sums, v, face, factor * (stars_of[face, rows, :] + star[rows, :]))

    copies = [
        pltpu.make_async_copy(
            sums.at[block], out_hbm.at[:, :, pl.ds(block * LANES, LANES)], sems.at[block]
        )
        for block in range(chunks)
    ]
    for copy in copies:
        copy.start()
    for copy in copies:
        copy.wait()


def body(
    state, step_size, levels, send_faces, partner, mortar_in, mortar_dir, return_faces, flux_source
):
    elems = state.shape[2]
    peers, slots = send_faces.shape
    hop = peers // 2
    count = mortar_dir.shape[0]
    base = 6 * elems + 1
    chunks = elems // LANES
    if slots != LANES or 4 * return_faces.shape[1] != LANES or 3 * count > LANES:
        raise ValueError("sizes")
    volume, spread, gather = operator_tables()
    volume = jnp.asarray(np.concatenate(split_table(volume), axis=0))
    spread, gather = jnp.asarray(spread), jnp.asarray(gather)
    way = mortar_dir.reshape(1, count)
    level = levels.reshape(1, elems)
    vmem = pl.BlockSpec(memory_space=pltpu.VMEM)
    smem = pl.BlockSpec(memory_space=pltpu.SMEM)
    hbm = pl.BlockSpec(memory_space=pl.ANY)
    lanes = pltpu.VMEM((chunks, 5, 64, LANES), F32)
    sems = pltpu.SemaphoreType.DMA((chunks,))
    grid = pltpu.VMEM((ROWS, LANES), jnp.int16)

    shapes = [
        jax.ShapeDtypeStruct((88, 2 * slots) if p in (0, hop) else (80, slots), F32)
        for p in range(peers)
    ]
    outgoing = pl.pallas_call(
        functools.partial(send_kernel, hop),
        out_shape=shapes,
        in_specs=[hbm] + [vmem] * 4,
        out_specs=[vmem] * peers,
        scratch_shapes=[
            lanes,
            pltpu.VMEM((6, 80, elems), F32),
            pltpu.VMEM((240, 4 * elems), BF16),
            pltpu.VMEM((8, count), F32),
            pltpu.VMEM((8, LANES), jnp.int32),
            grid,
            sems,
        ],
        name="send",
    )(state, send_faces, mortar_in, way, return_faces)
    arrived = []
    for peer in range(peers):
        distance = peer + 1 if peer < hop else hop - 1 - peer
        arrived.append(passed_along(outgoing[peer], "dev", distance))
    acc, traces, beside, big, own, ranges = pl.pallas_call(
        functools.partial(local_kernel, peers // 2),
        out_shape=[
            jax.ShapeDtypeStruct((chunks, 5, 64, LANES), F32),
            jax.ShapeDtypeStruct((80, 6 * elems), F32),
            jax.ShapeDtypeStruct((80, 6 * elems), F32),
            jax.ShapeDtypeStruct((80, 2 * LANES), F32),
            jax.ShapeDtypeStruct((80, LANES), F32),
            jax.ShapeDtypeStruct((16,), jnp.int32),
        ],
        in_specs=[hbm] + [vmem] * 4 + [smem, vmem],
        out_specs=[vmem] * 5 + [smem],
        scratch_shapes=[
            lanes,
            pltpu.VMEM((240, 6 * elems), BF16),
            pltpu.VMEM((8, 2 * LANES), jnp.int32),
            grid,
            sems,
        ],
        name="local",
    )(state, partner, mortar_in, flux_source, level, step_size, volume)
    return pl.pallas_call(
        functools.partial(finish_kernel, base, hop, peers),
        out_shape=jax.ShapeDtypeStruct((5, 64, elems), F32),
        in_specs=[vmem] * (peers + 11) + [smem, vmem, vmem, smem],
        out_specs=hbm,
        scratch_shapes=[
            lanes,
            pltpu.VMEM((6, 80, elems), F32),
            pltpu.VMEM((peers // 2, 240, 2 * slots), BF16),
            pltpu.VMEM((240, 3 * LANES), BF16),
            pltpu.VMEM((4, 80, elems), F32),
            pltpu.VMEM((2, 88, LANES), F32),
            pltpu.VMEM((8, 2 * LANES), jnp.int32),
            grid,
            sems,
        ],
        name="finish",
    )(
        *arrived,
        acc,
        traces,
        beside,
        big,
        own,
        partner,
        flux_source,
        send_faces,
        mortar_in,
        way,
        level,
        step_size,
        spread,
        gather,
        ranges,
    )


def solution(mesh):
    placed = (
        P(None, None, "dev"),
        P(),
        P("dev"),
        P("dev", None),
        P(None, "dev"),
        P(None, "dev"),
        P("dev"),
        P("dev", None),
        P(None, "dev"),
    )

    return jax.shard_map(
        body, mesh=mesh, in_specs=placed, out_specs=P(None, None, "dev"), check_vma=False
    )
```

profile of v0, /device:TPU:1, one launch (start us, length us, event | category | flops | bytes accessed | tf_op | source)
XLA Modules:
  0.0 33.5 jit_solution(17984029574526814149)
XLA Ops:
  0.0 3.4 %send.1 = (f32[88,256]{1,0:T(8,128)}, f32[80,128]{1,0:T(8,128)}, f32[80,128]{1,0:T(8,128)}, f32[80,128]{1,0:T(8,128)}, f32[88,256]{1,0:T(8,128)}, /*index=5*/f32...) custom-call(f32[5,64,512]{2,1,0:T(8,128)} %state_hbm.3, s32[8,128]{1,0:T(8,128)} %rest_15_.1, s32[5,40]{1,0:T(8,128)} %rest_16_.1, ...), custom_call_target="tpu_custom_call" | custom-call | tf_op jit(solution)/shard_map/send/pallas_call | solution.py:700
  3.4 2.6 %collective-permute-start = (f32[88,256]{1,0:T(8,128)}, f32[88,256]{1,0:T(8,128)S(1)}, u32[]{:S(2)}, u32[]{:S(2)}) collective-permute-start(f32[88,256]{1,0:T(8,128)} %get-tuple-element.19), channel_id=1, source_target_pairs={{31,0},{0,1},{1,2},{2,3},{3,4},{4,5},{5,6},{6,7},{7,8},{8,9},{9,10... | collective-permute-start | bytes 270344 | tf_op jit(solution)/shard_map/ppermute | solution.py:22
  6.0 0.0 collective-permute-start.4
  6.0 1.2 %collective-permute-start.1 = (f32[80,128]{1,0:T(8,128)}, f32[80,128]{1,0:T(8,128)S(1)}, u32[]{:S(2)}, u32[]{:S(2)}) collective-permute-start(f32[80,128]{1,0:T(8,128)} %get-tuple-element.20), channel_id=1, source_target_pairs={{30,0},{31,1},{0,2},{1,3},{2,4},{3,5},{4,6},{5,7},{6,8},{7,9},{8,1... | collective-permute-start | bytes 122888 | tf_op jit(solution)/shard_map/ppermute | solution.py:22
  7.2 2.1 %collective-permute-start.2 = (f32[80,128]{1,0:T(8,128)}, f32[80,128]{1,0:T(8,128)S(1)}, u32[]{:S(2)}, u32[]{:S(2)}) collective-permute-start(f32[80,128]{1,0:T(8,128)} %get-tuple-element.21), channel_id=1, source_target_pairs={{29,0},{30,1},{31,2},{0,3},{1,4},{2,5},{3,6},{4,7},{5,8},{6,9},{7,... | collective-permute-start | bytes 122888 | tf_op jit(solution)/shard_map/ppermute | solution.py:22
  9.3 1.5 %collective-permute-start.3 = (f32[80,128]{1,0:T(8,128)}, f32[80,128]{1,0:T(8,128)S(1)}, u32[]{:S(2)}, u32[]{:S(2)}) collective-permute-start(f32[80,128]{1,0:T(8,128)} %get-tuple-element.22), channel_id=1, source_target_pairs={{28,0},{29,1},{30,2},{31,3},{0,4},{1,5},{2,6},{3,7},{4,8},{5,9},{6... | collective-permute-start | bytes 122888 | tf_op jit(solution)/shard_map/ppermute | solution.py:22
  10.8 1.8 %collective-permute-done.1.rest_1_ = f32[80,128]{1,0:T(8,128)S(1)} collective-permute-done((f32[80,128]{1,0:T(8,128)}, f32[80,128]{1,0:T(8,128)S(1)}, u32[]{:S(2)}, u32[]{:S(2)}) %collective-permute-start.1) | collective-permute-done | bytes 40992 | tf_op jit(solution)/shard_map/ppermute | solution.py:22
  12.7 3.5 %collective-permute-start.5 = (f32[80,128]{1,0:T(8,128)}, f32[80,128]{1,0:T(8,128)S(1)}, u32[]{:S(2)}, u32[]{:S(2)}) collective-permute-start(f32[80,128]{1,0:T(8,128)} %get-tuple-element.24), channel_id=1, source_target_pairs={{2,0},{3,1},{4,2},{5,3},{6,4},{7,5},{8,6},{9,7},{10,8},{11,9},{12,... | collective-permute-start | bytes 122888 | tf_op jit(solution)/shard_map/ppermute | solution.py:22
  16.2 1.4 %collective-permute-done.2.rest_2_ = f32[80,128]{1,0:T(8,128)S(1)} collective-permute-done((f32[80,128]{1,0:T(8,128)}, f32[80,128]{1,0:T(8,128)S(1)}, u32[]{:S(2)}, u32[]{:S(2)}) %collective-permute-start.2) | collective-permute-done | bytes 40992 | tf_op jit(solution)/shard_map/ppermute | solution.py:22
  17.6 1.2 %collective-permute-start.6 = (f32[80,128]{1,0:T(8,128)}, f32[80,128]{1,0:T(8,128)S(1)}, u32[]{:S(2)}, u32[]{:S(2)}) collective-permute-start(f32[80,128]{1,0:T(8,128)} %get-tuple-element.25), channel_id=1, source_target_pairs={{3,0},{4,1},{5,2},{6,3},{7,4},{8,5},{9,6},{10,7},{11,8},{12,9},{13... | collective-permute-start | bytes 122888 | tf_op jit(solution)/shard_map/ppermute | solution.py:22
  18.8 0.0 collective-permute-done.3.rest_3_
  18.8 2.0 %collective-permute-start.7 = (f32[80,128]{1,0:T(8,128)}, f32[80,128]{1,0:T(8,128)S(1)}, u32[]{:S(2)}, u32[]{:S(2)}) collective-permute-start(f32[80,128]{1,0:T(8,128)} %get-tuple-element.26), channel_id=1, source_target_pairs={{4,0},{5,1},{6,2},{7,3},{8,4},{9,5},{10,6},{11,7},{12,8},{13,9},{1... | collective-permute-start | bytes 122888 | tf_op jit(solution)/shard_map/ppermute | solution.py:22
  21.4 5.3 %local.1 = (f32[4,5,64,128]{3,2,1,0:T(8,128)}, f32[80,3072]{1,0:T(8,128)}, f32[80,3072]{1,0:T(8,128)}, f32[80,256]{1,0:T(8,128)}, f32[80,128]{1,0:T(8,128)}, /*index=5*/s32[16]{0:T(128)}) custom-call(f32[5,64,512]{2,1,0:T(8,128)} %state_hbm.3, s32[6,512]{1,0:T(8,128)} %rest_13_.1, s32[5,40]{1,0:T(8,128)} %rest_16_.1, s32[6,512]{1,0:T(8,128)} %rest_14_.1, ...), custom_call_target="tpu_custom_call" | custom-call | tf_op jit(solution)/shard_map/local/pallas_call | solution.py:720
  26.7 0.0 copy-done.2
  26.7 0.0 copy-done.3
  26.7 0.0 copy-done.4
  26.7 0.0 collective-permute-done.5.rest_5_
  26.7 0.0 copy-start.5
  26.7 0.0 collective-permute-done.6.rest_6_
  26.7 0.0 copy-start.6
  26.8 0.0 collective-permute-done.7.rest_7_
  26.8 0.0 copy-start.7
  26.8 0.0 collective-permute-done.rest_0_
  26.8 0.0 copy-start
  26.8 0.0 collective-permute-done.4.rest_4_
  26.8 0.0 copy-start.1
  26.8 0.5 %copy-done.5 = f32[80,128]{1,0:T(8,128)} copy-done((f32[80,128]{1,0:T(8,128)}, f32[80,128]{1,0:T(8,128)S(1)}, u32[]{:S(2)}) %copy-start.5) | copy-done | bytes 40984
  27.3 0.0 copy-done.6
  27.4 0.0 copy-done.7
  27.4 0.1 copy-done
  27.5 0.0 copy-done.1
  27.5 6.0 %finish.1 = f32[5,64,512]{2,1,0:T(8,128)} custom-call(f32[88,256]{1,0:T(8,128)} %copy-done, f32[80,128]{1,0:T(8,128)} %copy-done.2, f32[80,128]{1,0:T(8,128)} %copy-done.3, f32[80,128]{1,0:T(8,128)} %copy-done.4, f32[88,256]{1,0:T(8,128)} %copy-done.1, f32[80,128]{1,0:T(8,128)} %copy-done.5, f32[80,128]{1,0:T(8,128)} %copy-done.6, f32[80,128]{1,0:T(8,128)} %copy-done.7, ...), custom_call_target="tpu_custom_call" | custom-call | tf_op jit(solution)/shard_map/finish/pallas_call | solution.py:741
  (3 shorter events, 0.0 us)
Async XLA Ops:
  3.4 23.4 %collective-permute-start = (f32[88,256]{1,0:T(8,128)}, f32[88,256]{1,0:T(8,128)S(1)}, u32[]{:S(2)}, u32[]{:S(2)}) collective-permute-start(f32[88,256]{1,0:T(8,128)} %get-tuple-element.19), channel_id=1, source_target_pairs={{31,0},{0,1},{1,2},{2,3},{3,4},{4,5},{5,6},{6,7},{7,8},{8,9},{9,10... | collective-permute-start | bytes 270344 | tf_op jit(solution)/shard_map/ppermute | solution.py:22
  6.0 20.8 %collective-permute-start.4 = (f32[88,256]{1,0:T(8,128)}, f32[88,256]{1,0:T(8,128)S(1)}, u32[]{:S(2)}, u32[]{:S(2)}) collective-permute-start(f32[88,256]{1,0:T(8,128)} %get-tuple-element.23), channel_id=1, source_target_pairs={{1,0},{2,1},{3,2},{4,3},{5,4},{6,5},{7,6},{8,7},{9,8},{10,9},{11,1... | collective-permute-start | bytes 270344 | tf_op jit(solution)/shard_map/ppermute | solution.py:22
  6.0 6.7 %collective-permute-start.1 = (f32[80,128]{1,0:T(8,128)}, f32[80,128]{1,0:T(8,128)S(1)}, u32[]{:S(2)}, u32[]{:S(2)}) collective-permute-start(f32[80,128]{1,0:T(8,128)} %get-tuple-element.20), channel_id=1, source_target_pairs={{30,0},{31,1},{0,2},{1,3},{2,4},{3,5},{4,6},{5,7},{6,8},{7,9},{8,1... | collective-permute-start | bytes 122888 | tf_op jit(solution)/shard_map/ppermute | solution.py:22
  7.2 10.4 %collective-permute-start.2 = (f32[80,128]{1,0:T(8,128)}, f32[80,128]{1,0:T(8,128)S(1)}, u32[]{:S(2)}, u32[]{:S(2)}) collective-permute-start(f32[80,128]{1,0:T(8,128)} %get-tuple-element.21), channel_id=1, source_target_pairs={{29,0},{30,1},{31,2},{0,3},{1,4},{2,5},{3,6},{4,7},{5,8},{6,9},{7,... | collective-permute-start | bytes 122888 | tf_op jit(solution)/shard_map/ppermute | solution.py:22
  9.3 9.5 %collective-permute-start.3 = (f32[80,128]{1,0:T(8,128)}, f32[80,128]{1,0:T(8,128)S(1)}, u32[]{:S(2)}, u32[]{:S(2)}) collective-permute-start(f32[80,128]{1,0:T(8,128)} %get-tuple-element.22), channel_id=1, source_target_pairs={{28,0},{29,1},{30,2},{31,3},{0,4},{1,5},{2,6},{3,7},{4,8},{5,9},{6... | collective-permute-start | bytes 122888 | tf_op jit(solution)/shard_map/ppermute | solution.py:22
  12.7 14.0 %copy-start.2 = (f32[80,128]{1,0:T(8,128)}, f32[80,128]{1,0:T(8,128)S(1)}, u32[]{:S(2)}) copy-start(f32[80,128]{1,0:T(8,128)S(1)} %collective-permute-done.1.rest_1_) | copy-start | bytes 122884
  12.7 14.1 %collective-permute-start.5 = (f32[80,128]{1,0:T(8,128)}, f32[80,128]{1,0:T(8,128)S(1)}, u32[]{:S(2)}, u32[]{:S(2)}) collective-permute-start(f32[80,128]{1,0:T(8,128)} %get-tuple-element.24), channel_id=1, source_target_pairs={{2,0},{3,1},{4,2},{5,3},{6,4},{7,5},{8,6},{9,7},{10,8},{11,9},{12,... | collective-permute-start | bytes 122888 | tf_op jit(solution)/shard_map/ppermute | solution.py:22
  17.6 9.1 %copy-start.3 = (f32[80,128]{1,0:T(8,128)}, f32[80,128]{1,0:T(8,128)S(1)}, u32[]{:S(2)}) copy-start(f32[80,128]{1,0:T(8,128)S(1)} %collective-permute-done.2.rest_2_) | copy-start | bytes 122884
  17.6 9.1 %collective-permute-start.6 = (f32[80,128]{1,0:T(8,128)}, f32[80,128]{1,0:T(8,128)S(1)}, u32[]{:S(2)}, u32[]{:S(2)}) collective-permute-start(f32[80,128]{1,0:T(8,128)} %get-tuple-element.25), channel_id=1, source_target_pairs={{3,0},{4,1},{5,2},{6,3},{7,4},{8,5},{9,6},{10,7},{11,8},{12,9},{13... | collective-permute-start | bytes 122888 | tf_op jit(solution)/shard_map/ppermute | solution.py:22
  18.8 7.9 %copy-start.4 = (f32[80,128]{1,0:T(8,128)}, f32[80,128]{1,0:T(8,128)S(1)}, u32[]{:S(2)}) copy-start(f32[80,128]{1,0:T(8,128)S(1)} %collective-permute-done.3.rest_3_) | copy-start | bytes 122884
  18.8 8.0 %collective-permute-start.7 = (f32[80,128]{1,0:T(8,128)}, f32[80,128]{1,0:T(8,128)S(1)}, u32[]{:S(2)}, u32[]{:S(2)}) collective-permute-start(f32[80,128]{1,0:T(8,128)} %get-tuple-element.26), channel_id=1, source_target_pairs={{4,0},{5,1},{6,2},{7,3},{8,4},{9,5},{10,6},{11,7},{12,8},{13,9},{1... | collective-permute-start | bytes 122888 | tf_op jit(solution)/shard_map/ppermute | solution.py:22
  26.7 0.6 %copy-start.5 = (f32[80,128]{1,0:T(8,128)}, f32[80,128]{1,0:T(8,128)S(1)}, u32[]{:S(2)}) copy-start(f32[80,128]{1,0:T(8,128)S(1)} %collective-permute-done.5.rest_5_) | copy-start | bytes 122884
  26.7 0.6 %copy-start.6 = (f32[80,128]{1,0:T(8,128)}, f32[80,128]{1,0:T(8,128)S(1)}, u32[]{:S(2)}) copy-start(f32[80,128]{1,0:T(8,128)S(1)} %collective-permute-done.6.rest_6_) | copy-start | bytes 122884
  26.8 0.6 %copy-start.7 = (f32[80,128]{1,0:T(8,128)}, f32[80,128]{1,0:T(8,128)S(1)}, u32[]{:S(2)}) copy-start(f32[80,128]{1,0:T(8,128)S(1)} %collective-permute-done.7.rest_7_) | copy-start | bytes 122884
  26.8 0.7 %copy-start = (f32[88,256]{1,0:T(8,128)}, f32[88,256]{1,0:T(8,128)S(1)}, u32[]{:S(2)}) copy-start(f32[88,256]{1,0:T(8,128)S(1)} %collective-permute-done.rest_0_) | copy-start | bytes 270340
  26.8 0.7 %copy-start.1 = (f32[88,256]{1,0:T(8,128)}, f32[88,256]{1,0:T(8,128)S(1)}, u32[]{:S(2)}) copy-start(f32[88,256]{1,0:T(8,128)S(1)} %collective-permute-done.4.rest_4_) | copy-start | bytes 270340
where the time goes:
time: 33.7 us; the launch traced here: 33.5 us
  Pallas kernels  14.7 us (44%)
  starting transfers between devices  14.1 us (42%)
  waiting for transfers between devices  3.29 us (10%)
  between operations  0.78 us (2%)
  local copies, waits for them, and re-layouts  0.67 us (2%)
    ppermute x8, starting transfers between devices, passed_along(): return lax.ppermute(block, axis, route)  14.1 us
    pallas_call x1, Pallas kernels, body(): pl.pallas_call(functools.partial(finish_kernel, base, hop, peers), out_sh...  6.03 us
    pallas_call x1, Pallas kernels, body(): pl.pallas_call(functools.partial(local_kernel, peers // 2), out_shape=[ja...  5.3 us
    pallas_call x1, Pallas kernels, body(): pl.pallas_call(functools.partial(send_kernel, hop), out_shape=shapes, in_...  3.35 us
    ppermute x8, waiting for transfers between devices, passed_along(): return lax.ppermute(block, axis, route)  3.29 us
  transfers between devices with their start and end apart: 8, of which 2 were waited for; matrix products, arithmetic and copies ran while one was open for 0% of the time, Pallas kernels for 16%

commit v1 on v0

--- a/solution.py
+++ b/solution.py
@@ -153,6 +153,16 @@
     return parts[0] if len(parts) == 1 else jnp.concatenate(parts, axis=0)
 
 
+def split_product(table_ref, value):
+    rows = table_ref.shape[0] // 3
+    high, middle, low = three_pieces(value)
+    first = jnp.dot(table_ref[...], high, preferred_element_type=F32)
+    second = jnp.dot(table_ref[0 : 2 * rows, :], middle, preferred_element_type=F32)
+    third = jnp.dot(table_ref[0:rows, :], low, preferred_element_type=F32)
+    small = (first[2 * rows :] + second[rows:]) + third
+    return first[0:rows] + ((first[rows : 2 * rows] + second[0:rows]) + small)
+
+
 def joined(product):
     return (product[0:80] + product[80:160]) + product[160:240]
 
@@ -202,16 +212,25 @@
     return jnp.max(value)
 
 
-def send_kernel(hop, state_hbm, faces_ref, mortar_ref, way_ref, back_ref, *rest):
-    peers, slots = faces_ref.shape
-    outs = rest[:peers]
-    lanes, traces, pieces, table, spots, grid, sems = rest[peers:]
-    elems = state_hbm.shape[2]
+def send_kernel(hop, peers, *rest):
+    inputs, outs, held = rest[:11], rest[11 : 11 + peers], rest[11 + peers : 21 + peers]
+    traces, pieces, table, spots, grid, back_ref, sems, state_sems = rest[21 + peers :]
+    lanes, faces_ref, mortar_ref, way_ref = held[:4]
+    elems = inputs[0].shape[2]
     chunks = elems // LANES
+    targets = [faces_ref, mortar_ref, way_ref, back_ref] + list(held[4:])
+    loads = [
+        pltpu.make_async_copy(source, target, sems.at[k])
+        for k, (source, target) in enumerate(zip(inputs[1:], targets))
+    ]
+    copies = read_lanes(inputs[0], lanes, state_sems)
+    for copy in loads[:4] + copies + loads[4:]:
+        copy.start()
+    slots = faces_ref.shape[1]
     count, backs = mortar_ref.shape[1], back_ref.shape[1]
-    copies = read_lanes(state_hbm, lanes, sems)
-    for copy in copies:
-        copy.start()
+    number_rows(grid)
+    for copy in loads[:4]:
+        copy.wait()
 
     wanted = [faces_ref[p : p + 1, :] for p in range(peers)]
     faces = faces_ref[...]
@@ -222,7 +241,6 @@
     starts = [least[p, 0] for p in range(peers)]
     stops = [most[p, 0] for p in range(peers)]
 
-    number_rows(grid)
     table[...] = jnp.zeros(table.shape, F32)
     table[0:5, :] = mortar_ref[...].astype(F32)
     table[5:6, :] = way_ref[...].astype(F32)
@@ -306,15 +324,17 @@
     def _(step):
         collect(step, False)
 
+    for copy in loads[4:]:
+        copy.wait()
+
 
 def local_kernel(
     block_count,
-    state_hbm,
+    lanes,
     partner_ref,
     mortar_ref,
     source_ref,
     level_ref,
-    step_ref,
     volume_ref,
     acc_ref,
     traces_ref,
@@ -322,13 +342,11 @@
     big_ref,
     own_ref,
     range_ref,
-    lanes,
     pieces,
     spots,
     grid,
-    sems,
 ):
-    elems = state_hbm.shape[2]
+    elems = partner_ref.shape[1]
     chunks = elems // LANES
     count = mortar_ref.shape[1]
     wide = 2 * LANES
@@ -341,9 +359,6 @@
         range_ref[face] = jnp.minimum(least[face, 0], block_count - 1)
         range_ref[8 + face] = most[face, 0]
     range_ref[6] = highest(jnp.where(most > least, 1, 0))
-    copies = read_lanes(state_hbm, lanes, sems)
-    for copy in copies:
-        copy.start()
     returned = own_ref.shape[1] // 2
     first_back = 5 * count + 1
     slot = lax.broadcasted_iota(jnp.int32, (returned, elems), 0) + first_back
@@ -352,16 +367,14 @@
     for face in range(4):
         hit = jnp.where(source_ref[face : face + 1, :] == slot, number + (face * elems + 1), hit)
     column = jnp.sum(hit.astype(F32), axis=1, keepdims=True)
-    corner = lax.broadcasted_iota(jnp.int32, (returned, LANES), 0) == lax.broadcasted_iota(
-        jnp.int32, (returned, LANES), 1
+    corner = lax.broadcasted_iota(jnp.int32, (returned, LANES), 0) + count == (
+        lax.broadcasted_iota(jnp.int32, (returned, LANES), 1)
     )
     owner = jnp.sum(jnp.where(corner, column, 0.0), axis=0, keepdims=True).astype(jnp.int32) - 1
     spots[...] = jnp.full(spots.shape, -1, jnp.int32)
     for row, place in enumerate(packed_places(count)):
         spots[0:1, place : place + count] = mortar_ref[row : row + 1, :]
 
-    for copy in copies:
-        copy.wait()
     for face in range(6):
         for var in range(5):
             rows = slice(16 * var, 16 * var + 16)
@@ -371,8 +384,23 @@
                     face * elems + block * LANES, face * elems + (block + 1) * LANES
                 )
                 traces_ref[rows, columns] = part
-                store_pieces(pieces, 16 * var, columns, part)
-    for face in range(6):
+                if face < 4:
+                    store_pieces(pieces, 16 * var, columns, part)
+
+    def lane_gathered(wanted, first, last, out, column):
+        spot = jnp.broadcast_to(jnp.bitwise_and(wanted, LANES - 1), (8, LANES))
+        chunk_of = jnp.broadcast_to(lax.shift_right_arithmetic(wanted, 7), (8, LANES))
+        for r in range(10):
+            rows = slice(8 * r, 8 * r + 8)
+            value = jnp.zeros((8, LANES), F32)
+            for chunk in range(first, last):
+                part = traces_ref[rows, chunk * LANES : (chunk + 1) * LANES]
+                value = jnp.where(
+                    chunk_of == chunk, jnp.take_along_axis(part, spot, axis=1), value
+                )
+            out[rows, column : column + LANES] = value
+
+    def matrix_gathered(face):
         other = (face ^ 1) * elems
         product = jnp.dot(
             pieces[:, other : other + elems],
@@ -380,16 +408,27 @@
             preferred_element_type=F32,
         )
         beside_ref[:, face * elems : (face + 1) * elems] = joined(product)
+
     wanted = spots[0:1, :]
+    for face in range(4):
+        matrix_gathered(face)
+        if face < 2:
+            for block in range(chunks):
+                columns = slice(block * LANES, (block + 1) * LANES)
+                first = ((4 + face) ^ 1) * chunks
+                lane_gathered(
+                    partner_ref[4 + face : 5 + face, columns],
+                    first,
+                    first + chunks,
+                    beside_ref,
+                    (4 + face) * elems + block * LANES,
+                )
+        if face == 2:
+            lane_gathered(owner, 0, 4 * chunks, own_ref, 0)
     big_ref[...] = joined(
-        jnp.dot(
-            pieces[:, 0 : 4 * elems], one_hot(grid, wanted, 4 * elems), preferred_element_type=F32
-        )
-    )
-    own_ref[...] = joined(
-        jnp.dot(pieces[:, 0 : 4 * elems], one_hot(grid, owner, 4 * elems), preferred_element_type=F32)
-    )
-    factor = -step_ref[0] * jnp.left_shift(2, level_ref[...]).astype(F32)
+        jnp.dot(pieces[...], one_hot(grid, wanted, 4 * elems), preferred_element_type=F32)
+    )
+    factor = -(jnp.left_shift(2, level_ref[...]).astype(F32))
     cons = [
         jnp.concatenate([lanes[block, v] for block in range(chunks)], axis=1) for v in range(5)
     ]
@@ -397,14 +436,7 @@
     fluxes = [axis_flux(cons, prim, axis, 1) for axis in range(3)]
     for var in range(5):
         stacked = jnp.concatenate([fluxes[axis][var] for axis in range(3)], axis=0)
-        high, middle, low = three_pieces(stacked)
-        first = jnp.dot(volume_ref[...], high, preferred_element_type=F32)
-        second = jnp.dot(volume_ref[0:128, :], middle, preferred_element_type=F32)
-        third = jnp.dot(volume_ref[0:64, :], low, preferred_element_type=F32)
-        total = factor * (
-            first[0:64]
-            + ((first[64:128] + second[0:64]) + ((first[128:192] + second[64:128]) + third))
-        )
+        total = factor * split_product(volume_ref, stacked)
         for block in range(chunks):
             acc_ref[block, var] = total[:, block * LANES : (block + 1) * LANES]
 
@@ -418,33 +450,6 @@
         ],
         axis=0,
     )
-
-
-def mortar_stars(traces, way, spread, gather):
-    normal = [
-        (way == 2 * axis + 1).astype(F32) - (way == 2 * axis).astype(F32) for axis in range(3)
-    ]
-    near = jnp.dot(spread, traces[0], preferred_element_type=F32, precision=HIGHEST)
-    stars = []
-    for quarter in range(4):
-        first = [near[80 * quarter + 16 * v : 80 * quarter + 16 * v + 16] for v in range(5)]
-        second = [traces[1 + quarter][16 * v : 16 * v + 16] for v in range(5)]
-        first_flux, first_speed = normal_flux(first, normal)
-        second_flux, second_speed = normal_flux(second, normal)
-        speed = jnp.maximum(first_speed, second_speed)
-        stars.append(
-            jnp.concatenate(
-                [
-                    0.5 * (first_flux[v] + second_flux[v]) - 0.5 * speed * (second[v] - first[v])
-                    for v in range(5)
-                ],
-                axis=0,
-            )
-        )
-    whole = jnp.dot(
-        gather, jnp.concatenate(stars, axis=0), preferred_element_type=F32, precision=HIGHEST
-    )
-    return whole, stars
 
 
 def finish_kernel(base, hop, peers, *rest):
@@ -547,8 +552,9 @@
                 )
 
     factor = (-6.0 * step_ref[0]) * jnp.left_shift(2, level_ref[...]).astype(F32)
-    sums[...] = acc_ref[...]
-    for face in range(6):
+    sums[...] = step_ref[0] * acc_ref[...]
+
+    def conform(face):
         axis, sign = face // 2, 2 * (face % 2) - 1
         columns = slice(face * elems, (face + 1) * elems)
         block = range_ref[face]
@@ -578,76 +584,102 @@
             else:
                 add_face(sums, v, face, factor * jump)
 
-    spots[...] = jnp.full(spots.shape, empty, jnp.int32)
-    for row, place in enumerate(places):
-        spots[0:1, place : place + count] = mortar_ref[row : row + 1, :]
-    spots[1:2, 0:count] = way_ref[...]
-    packed = spots[0:1, :]
-    total = jnp.zeros((240, wide), F32)
-    for block in range(peers // 2):
-        total = total + jnp.dot(
-            pieces[block],
-            one_hot(grid, packed - (base + block * wide), wide),
-            preferred_element_type=F32,
-        )
-    both = with_reference(joined(total) + big_ref[...], packed == empty)
-    local = []
-    for row, place in enumerate(places):
-        part = both[:, 0:LANES] if place < LANES else both[:, LANES:]
-        shift = place % LANES
-        local.append(part if shift == 0 else pltpu.roll(part, LANES - shift, 1))
-    lane = lax.broadcasted_iota(jnp.int32, (1, LANES), 1)
-    used = lane < count
-    local = [with_reference(part, jnp.logical_not(used)) for part in local]
-    local_way = jnp.where(used, spots[1:2, 0:LANES], 0)
-
-    moved = []
-    for group in range(4):
-        shift = group * backs
-        parts = [
-            payload[0] if shift == 0 else pltpu.roll(payload[0], LANES - shift, 1),
-            payload[1] if shift == backs else pltpu.roll(payload[1], (backs - shift) % LANES, 1),
+    def mortar():
+        spots[...] = jnp.full(spots.shape, empty, jnp.int32)
+        for row, place in enumerate(places):
+            spots[0:1, place : place + count] = mortar_ref[row : row + 1, :]
+        spots[1:2, 0:count] = way_ref[...]
+        packed = spots[0:1, :]
+        total = jnp.zeros((240, wide), F32)
+        for block in range(peers // 2):
+            total = total + jnp.dot(
+                pieces[block],
+                one_hot(grid, packed - (base + block * wide), wide),
+                preferred_element_type=F32,
+            )
+        both = joined(total) + big_ref[...]
+        yield
+        lane = lax.broadcasted_iota(jnp.int32, (1, LANES), 1)
+        mine = lane < count
+        backs_end = count + 2 * backs
+        own = own_ref[...]
+        moved = []
+        for group in range(4):
+            shift = group * backs
+            parts = [
+                pltpu.roll(payload[side], (count + side * backs - shift) % LANES, 1)
+                for side in range(2)
+            ]
+            moved.append(jnp.where(lane < count + backs, parts[0], parts[1]))
+        unused = (lane >= backs_end) | ((lane >= count) & (own[0:1] == 0.0))
+        unused = unused | (mine & (packed[:, 0:LANES] == empty))
+        kind = jnp.where(mine, 0, moved[0][81:82].astype(jnp.int32))
+        way = jnp.where(mine, spots[1:2, 0:LANES], moved[0][82:83].astype(jnp.int32))
+        large = kind == 0
+        traces = []
+        for row, place in enumerate(places):
+            part = both[:, 0:LANES] if place < LANES else both[:, LANES:]
+            shift = place % LANES
+            part = part if shift == 0 else pltpu.roll(part, LANES - shift, 1)
+            if row == 0:
+                back = jnp.where(large, own, moved[0][0:80])
+            else:
+                back = jnp.where(large, moved[row - 1][0:80], own)
+            traces.append(with_reference(jnp.where(mine, part, back), unused))
+        normal = [
+            (way == 2 * axis + 1).astype(F32) - (way == 2 * axis).astype(F32) for axis in range(3)
         ]
-        moved.append(jnp.where(lane < backs, parts[0], parts[1]))
-    own = own_ref[...]
-    unused = (lane >= 2 * backs) | (own[0:1] == 0.0)
-    kind = jnp.where(unused, 0, moved[0][81:82].astype(jnp.int32))
-    back_way = jnp.where(unused, 0, moved[0][82:83].astype(jnp.int32))
-    large = kind == 0
-    back = [jnp.where(large, own, moved[0][0:80])]
-    for quarter in range(4):
-        back.append(jnp.where(large, moved[quarter][0:80], own))
-    back = [with_reference(part, unused) for part in back]
-
-    traces = [jnp.concatenate([local[k], back[k]], axis=1) for k in range(5)]
-    way = jnp.concatenate([local_way, back_way], axis=1)
-    whole, stars = mortar_stars(traces, way, spread_ref[...], gather_ref[...])
-    values = [whole[:, 0:LANES]] + [-star[:, 0:LANES] for star in stars]
-    result = whole[:, LANES:]
-    for quarter in range(4):
-        result = jnp.where(kind == 1 + quarter, -stars[quarter][:, LANES:], result)
-    halves = [jnp.zeros((80, LANES), F32), jnp.zeros((80, LANES), F32)]
-    for row, place in enumerate(places):
-        shift = place % LANES
-        part = values[row] if shift == 0 else pltpu.roll(values[row], shift, 1)
-        inside = (lane >= shift) & (lane < shift + count)
-        halves[place // LANES] = jnp.where(inside, part, halves[place // LANES])
-    for which, value in enumerate(halves + [result]):
-        store_pieces(fluxes, 0, slice(which * LANES, (which + 1) * LANES), value[0:16])
-        for var in range(1, 5):
-            store_pieces(
-                fluxes,
-                16 * var,
-                slice(which * LANES, (which + 1) * LANES),
-                value[16 * var : 16 * var + 16],
+        near = split_product(spread_ref, traces[0])
+        yield
+        stars = []
+        for quarter in range(4):
+            first = [near[80 * quarter + 16 * v : 80 * quarter + 16 * v + 16] for v in range(5)]
+            second = [traces[1 + quarter][16 * v : 16 * v + 16] for v in range(5)]
+            first_flux, first_speed = normal_flux(first, normal)
+            second_flux, second_speed = normal_flux(second, normal)
+            speed = jnp.maximum(first_speed, second_speed)
+            stars.append(
+                jnp.concatenate(
+                    [
+                        0.5 * (first_flux[v] + second_flux[v])
+                        - 0.5 * speed * (second[v] - first[v])
+                        for v in range(5)
+                    ],
+                    axis=0,
+                )
             )
+            if quarter == 1:
+                yield
+        whole = split_product(gather_ref, jnp.concatenate(stars, axis=0))
+        yield
+        values = [whole] + [-star for star in stars]
+        result = whole
+        for quarter in range(4):
+            result = jnp.where(kind == 1 + quarter, values[1 + quarter], result)
+        halves = [jnp.zeros((80, LANES), F32), jnp.zeros((80, LANES), F32)]
+        for row, place in enumerate(places):
+            shift = place % LANES
+            part = values[row] if shift == 0 else pltpu.roll(values[row], shift, 1)
+            inside = (lane >= shift) & (lane < shift + count)
+            halves[place // LANES] = jnp.where(inside, part, halves[place // LANES])
+        for which, value in enumerate(halves + [result]):
+            columns = slice(which * LANES, (which + 1) * LANES)
+            for var in range(5):
+                store_pieces(fluxes, 16 * var, columns, value[16 * var : 16 * var + 16])
+
+    chain = mortar()
+    for face in (4, 5, 0, 1, 2, 3):
+        next(chain, None)
+        conform(face)
+    for _ in chain:
+        pass
 
     for face in range(4):
         entry = sources[face]
         row = sum((entry >= (k + 1) * count).astype(jnp.int32) for k in range(4))
         spot = entry - row * count
         column = jnp.where(row >= 3, LANES + (row - 3) * count, row * count) + spot
-        beyond = 2 * LANES + entry - (5 * count + 1)
+        beyond = 2 * LANES + count + entry - (5 * count + 1)
         column = jnp.where(entry < 5 * count, column, jnp.where(entry > 5 * count, beyond, -1))
         star = joined(
             jnp.dot(
@@ -679,17 +711,18 @@
     count = mortar_dir.shape[0]
     base = 6 * elems + 1
     chunks = elems // LANES
-    if slots != LANES or 4 * return_faces.shape[1] != LANES or 3 * count > LANES:
+    backs = return_faces.shape[1]
+    if slots != LANES or 4 * backs != LANES or max(3 * count, count + 2 * backs) > LANES:
         raise ValueError("sizes")
-    volume, spread, gather = operator_tables()
-    volume = jnp.asarray(np.concatenate(split_table(volume), axis=0))
-    spread, gather = jnp.asarray(spread), jnp.asarray(gather)
+    volume, spread, gather = (
+        jnp.asarray(np.concatenate(split_table(t), axis=0)) for t in operator_tables()
+    )
     way = mortar_dir.reshape(1, count)
     level = levels.reshape(1, elems)
     vmem = pl.BlockSpec(memory_space=pltpu.VMEM)
     smem = pl.BlockSpec(memory_space=pltpu.SMEM)
-    hbm = pl.BlockSpec(memory_space=pl.ANY)
-    lanes = pltpu.VMEM((chunks, 5, 64, LANES), F32)
+    hbm = pl.BlockSpec(memory_space=pltpu.HBM)
+    lanes = jax.ShapeDtypeStruct((chunks, 5, 64, LANES), F32)
     sems = pltpu.SemaphoreType.DMA((chunks,))
     grid = pltpu.VMEM((ROWS, LANES), jnp.int16)
 
@@ -697,22 +730,32 @@
         jax.ShapeDtypeStruct((88, 2 * slots) if p in (0, hop) else (80, slots), F32)
         for p in range(peers)
     ]
-    outgoing = pl.pallas_call(
-        functools.partial(send_kernel, hop),
-        out_shape=shapes,
-        in_specs=[hbm] + [vmem] * 4,
-        out_specs=[vmem] * peers,
+    inputs = [state, send_faces, mortar_in, way, return_faces, partner, flux_source, level]
+    inputs += [volume, spread, gather]
+    held = [lanes] + [
+        jax.ShapeDtypeStruct(x.shape, x.dtype) for x in inputs[1:4] + inputs[5:]
+    ]
+    results = pl.pallas_call(
+        functools.partial(send_kernel, hop, peers),
+        out_shape=shapes + held,
+        in_specs=[hbm] * len(inputs),
+        out_specs=[vmem] * (peers + len(held)),
         scratch_shapes=[
-            lanes,
             pltpu.VMEM((6, 80, elems), F32),
             pltpu.VMEM((240, 4 * elems), BF16),
             pltpu.VMEM((8, count), F32),
             pltpu.VMEM((8, LANES), jnp.int32),
             grid,
+            pltpu.VMEM(return_faces.shape, jnp.int32),
+            pltpu.SemaphoreType.DMA((len(inputs) - 1,)),
             sems,
         ],
         name="send",
-    )(state, send_faces, mortar_in, way, return_faces)
+        compiler_params=pltpu.CompilerParams(vmem_limit_bytes=14 << 20),
+    )(*[pltpu.with_memory_space_constraint(x, pltpu.HBM) for x in inputs])
+    outgoing = results[:peers]
+    state, send_faces, mortar_in, way, partner, flux_source, level = results[peers : peers + 7]
+    volume, spread, gather = results[peers + 7 :]
     arrived = []
     for peer in range(peers):
         distance = peer + 1 if peer < hop else hop - 1 - peer
@@ -720,31 +763,30 @@
     acc, traces, beside, big, own, ranges = pl.pallas_call(
         functools.partial(local_kernel, peers // 2),
         out_shape=[
-            jax.ShapeDtypeStruct((chunks, 5, 64, LANES), F32),
+            lanes,
             jax.ShapeDtypeStruct((80, 6 * elems), F32),
             jax.ShapeDtypeStruct((80, 6 * elems), F32),
             jax.ShapeDtypeStruct((80, 2 * LANES), F32),
             jax.ShapeDtypeStruct((80, LANES), F32),
             jax.ShapeDtypeStruct((16,), jnp.int32),
         ],
-        in_specs=[hbm] + [vmem] * 4 + [smem, vmem],
+        in_specs=[vmem] * 6,
         out_specs=[vmem] * 5 + [smem],
         scratch_shapes=[
-            lanes,
-            pltpu.VMEM((240, 6 * elems), BF16),
+            pltpu.VMEM((240, 4 * elems), BF16),
             pltpu.VMEM((8, 2 * LANES), jnp.int32),
             grid,
-            sems,
         ],
         name="local",
-    )(state, partner, mortar_in, flux_source, level, step_size, volume)
+        compiler_params=pltpu.CompilerParams(vmem_limit_bytes=14 << 20),
+    )(state, partner, mortar_in, flux_source, level, volume)
     return pl.pallas_call(
         functools.partial(finish_kernel, base, hop, peers),
         out_shape=jax.ShapeDtypeStruct((5, 64, elems), F32),
         in_specs=[vmem] * (peers + 11) + [smem, vmem, vmem, smem],
         out_specs=hbm,
         scratch_shapes=[
-            lanes,
+            pltpu.VMEM(lanes.shape, F32),
             pltpu.VMEM((6, 80, elems), F32),
             pltpu.VMEM((peers // 2, 240, 2 * slots), BF16),
             pltpu.VMEM((240, 3 * LANES), BF16),
@@ -755,6 +797,7 @@
             sems,
         ],
         name="finish",
+        compiler_params=pltpu.CompilerParams(vmem_limit_bytes=14 << 20),
     )(
         *arrived,
         acc,

time: 33.7 us -> 26.1 us (0.77)
  Pallas kernels: 14.7 us -> 8.09 us
  local copies, waits for them, and re-layouts: 0.67 us -> 0 us
  waiting for transfers between devices: 3.29 us -> 2.87 us
    pallas_call x2, Pallas kernels: 8.66 us -> 4.15 us  [the longest x1 2.24 us: body(): pl.pallas_call(functools.partial(send_kernel, hop, peers), out_shape=shap...]
    pallas_call x1, Pallas kernels: 6.03 us -> 3.95 us  [body(): pl.pallas_call(functools.partial(finish_kernel, base, hop, peers), out_sh...]
    unnamed x16 -> x0, local copies, waits for them, and re-layouts: 0.67 us -> none
    ppermute x8, waiting for transfers between devices: 3.29 us -> 2.87 us  [passed_along(): return lax.ppermute(block, axis, route)]
  transfers between devices with their start and end apart: 8 -> 8, of which waited for: 2 -> 2; matrix products, arithmetic and copies ran while one was open for 0% -> 0% of each run, Pallas kernels for 16% -> 7%
where the time goes in v1:
time: 26.1 us; the launch traced here: 25.9 us
  starting transfers between devices  14.3 us (55%)
  Pallas kernels  8.09 us (31%)
  waiting for transfers between devices  2.87 us (11%)
  between operations  0.71 us (3%)
    ppermute x8, starting transfers between devices, passed_along(): return lax.ppermute(block, axis, route)  14.3 us
    pallas_call x1, Pallas kernels, body(): pl.pallas_call(functools.partial(finish_kernel, base, hop, peers), out_sh...  3.95 us
    ppermute x8, waiting for transfers between devices, passed_along(): return lax.ppermute(block, axis, route)  2.87 us
    pallas_call x1, Pallas kernels, body(): pl.pallas_call(functools.partial(send_kernel, hop, peers), out_shape=shap...  2.24 us
    pallas_call x1, Pallas kernels, body(): pl.pallas_call(functools.partial(local_kernel, peers // 2), out_shape=[la...  1.91 us
  transfers between devices with their start and end apart: 8, of which 2 were waited for; matrix products, arithmetic and copies ran while one was open for 0% of the time, Pallas kernels for 7%

profile of v1, /device:TPU:1, one launch (start us, length us, event | category | flops | bytes accessed | tf_op | source)
XLA Modules:
  0.0 25.9 jit_solution(1437107090757877112)
XLA Ops:
  0.0 2.2 %send.1 = (f32[88,256]{1,0:T(8,128)S(1)}, f32[80,128]{1,0:T(8,128)S(1)}, f32[80,128]{1,0:T(8,128)S(1)}, f32[80,128]{1,0:T(8,128)S(1)}, f32[88,256]{1,0:T(8,128)S...) custom-call(f32[5,64,512]{2,1,0:T(8,128)} %rest_0_.1, ...), custom_call_target="tpu_custom_call" | custom-call | tf_op jit(solution)/shard_map/send/pallas_call | solution.py:738
  2.2 2.6 %collective-permute-start = (f32[88,256]{1,0:T(8,128)S(1)}, f32[88,256]{1,0:T(8,128)S(1)}, u32[]{:S(2)}, u32[]{:S(2)}) collective-permute-start(f32[88,256]{1,0:T(8,128)S(1)} %get-tuple-element.29), channel_id=1, source_target_pairs={{31,0},{0,1},{1,2},{2,3},{3,4},{4,5},{5,6},{6,7},{7,8},{8,9},{9,10... | collective-permute-start | bytes 270344 | tf_op jit(solution)/shard_map/ppermute | solution.py:22
  4.9 0.0 collective-permute-start.4
  4.9 1.2 %collective-permute-start.1 = (f32[80,128]{1,0:T(8,128)S(1)}, f32[80,128]{1,0:T(8,128)S(1)}, u32[]{:S(2)}, u32[]{:S(2)}) collective-permute-start(f32[80,128]{1,0:T(8,128)S(1)} %get-tuple-element.30), channel_id=1, source_target_pairs={{30,0},{31,1},{0,2},{1,3},{2,4},{3,5},{4,6},{5,7},{6,8},{7,9},{8,1... | collective-permute-start | bytes 122888 | tf_op jit(solution)/shard_map/ppermute | solution.py:22
  6.1 2.0 %collective-permute-start.2 = (f32[80,128]{1,0:T(8,128)S(1)}, f32[80,128]{1,0:T(8,128)S(1)}, u32[]{:S(2)}, u32[]{:S(2)}) collective-permute-start(f32[80,128]{1,0:T(8,128)S(1)} %get-tuple-element.31), channel_id=1, source_target_pairs={{29,0},{30,1},{31,2},{0,3},{1,4},{2,5},{3,6},{4,7},{5,8},{6,9},{7,... | collective-permute-start | bytes 122888 | tf_op jit(solution)/shard_map/ppermute | solution.py:22
  8.2 1.6 %collective-permute-start.3 = (f32[80,128]{1,0:T(8,128)S(1)}, f32[80,128]{1,0:T(8,128)S(1)}, u32[]{:S(2)}, u32[]{:S(2)}) collective-permute-start(f32[80,128]{1,0:T(8,128)S(1)} %get-tuple-element.32), channel_id=1, source_target_pairs={{28,0},{29,1},{30,2},{31,3},{0,4},{1,5},{2,6},{3,7},{4,8},{5,9},{6... | collective-permute-start | bytes 122888 | tf_op jit(solution)/shard_map/ppermute | solution.py:22
  9.7 1.6 %collective-permute-done.1.rest_1_ = f32[80,128]{1,0:T(8,128)S(1)} collective-permute-done((f32[80,128]{1,0:T(8,128)S(1)}, f32[80,128]{1,0:T(8,128)S(1)}, u32[]{:S(2)}, u32[]{:S(2)}) %collective-permute-start.1) | collective-permute-done | bytes 40992 | tf_op jit(solution)/shard_map/ppermute | solution.py:22
  11.3 3.7 %collective-permute-start.5 = (f32[80,128]{1,0:T(8,128)S(1)}, f32[80,128]{1,0:T(8,128)S(1)}, u32[]{:S(2)}, u32[]{:S(2)}) collective-permute-start(f32[80,128]{1,0:T(8,128)S(1)} %get-tuple-element.34), channel_id=1, source_target_pairs={{2,0},{3,1},{4,2},{5,3},{6,4},{7,5},{8,6},{9,7},{10,8},{11,9},{12,... | collective-permute-start | bytes 122888 | tf_op jit(solution)/shard_map/ppermute | solution.py:22
  15.1 1.2 %collective-permute-done.2.rest_2_ = f32[80,128]{1,0:T(8,128)S(1)} collective-permute-done((f32[80,128]{1,0:T(8,128)S(1)}, f32[80,128]{1,0:T(8,128)S(1)}, u32[]{:S(2)}, u32[]{:S(2)}) %collective-permute-start.2) | collective-permute-done | bytes 40992 | tf_op jit(solution)/shard_map/ppermute | solution.py:22
  16.3 1.2 %collective-permute-start.6 = (f32[80,128]{1,0:T(8,128)S(1)}, f32[80,128]{1,0:T(8,128)S(1)}, u32[]{:S(2)}, u32[]{:S(2)}) collective-permute-start(f32[80,128]{1,0:T(8,128)S(1)} %get-tuple-element.35), channel_id=1, source_target_pairs={{3,0},{4,1},{5,2},{6,3},{7,4},{8,5},{9,6},{10,7},{11,8},{12,9},{13... | collective-permute-start | bytes 122888 | tf_op jit(solution)/shard_map/ppermute | solution.py:22
  17.4 0.0 collective-permute-done.3.rest_3_
  17.4 1.9 %collective-permute-start.7 = (f32[80,128]{1,0:T(8,128)S(1)}, f32[80,128]{1,0:T(8,128)S(1)}, u32[]{:S(2)}, u32[]{:S(2)}) collective-permute-start(f32[80,128]{1,0:T(8,128)S(1)} %get-tuple-element.36), channel_id=1, source_target_pairs={{4,0},{5,1},{6,2},{7,3},{8,4},{9,5},{10,6},{11,7},{12,8},{13,9},{1... | collective-permute-start | bytes 122888 | tf_op jit(solution)/shard_map/ppermute | solution.py:22
  20.0 1.9 %local.1 = (f32[4,5,64,128]{3,2,1,0:T(8,128)S(1)}, f32[80,3072]{1,0:T(8,128)S(1)}, f32[80,3072]{1,0:T(8,128)S(1)}, f32[80,256]{1,0:T(8,128)S(1)}, f32[80,128]{1,0:T(8,128)S(1)}, /*index=5*/s32[16]{0:T(128)S(1)}) custom-call(f32[4,5,64,128]{3,2,1,0:T(8,128)S(1)} %get-tuple-element.37.lanes, s32[6,512]{1,0:T(8,128)S(1)} %get-tuple-element.38.partner_ref.rest_13_, ...), custom_call_target="tpu_custom_call" | custom-call | tf_op jit(solution)/shard_map/local/pallas_call | solution.py:763
  21.9 0.0 collective-permute-done.5.rest_5_
  21.9 0.0 collective-permute-done.6.rest_6_
  22.0 0.0 collective-permute-done.7.rest_7_
  22.0 0.0 collective-permute-done.rest_0_
  22.0 0.0 collective-permute-done.4.rest_4_
  22.0 3.9 %finish.1 = f32[5,64,512]{2,1,0:T(8,128)} custom-call(f32[88,256]{1,0:T(8,128)S(1)} %collective-permute-done.rest_0_, f32[80,128]{1,0:T(8,128)S(1)} %collective-permute-done.1.rest_1_, f32[80,128]{1,0:T(8,128)S(1)} %collective-permute-done.2.rest_2_, f32[80,128]{1,0:T(8,128)S(1)} %collective-permute-done.3.rest_3_, ...), custom_call_target="tpu_custom_call" | custom-call | tf_op jit(solution)/shard_map/finish/pallas_call | solution.py:783
Async XLA Ops:
  2.2 19.7 %collective-permute-start = (f32[88,256]{1,0:T(8,128)S(1)}, f32[88,256]{1,0:T(8,128)S(1)}, u32[]{:S(2)}, u32[]{:S(2)}) collective-permute-start(f32[88,256]{1,0:T(8,128)S(1)} %get-tuple-element.29), channel_id=1, source_target_pairs={{31,0},{0,1},{1,2},{2,3},{3,4},{4,5},{5,6},{6,7},{7,8},{8,9},{9,10... | collective-permute-start | bytes 270344 | tf_op jit(solution)/shard_map/ppermute | solution.py:22
  4.9 17.1 %collective-permute-start.4 = (f32[88,256]{1,0:T(8,128)S(1)}, f32[88,256]{1,0:T(8,128)S(1)}, u32[]{:S(2)}, u32[]{:S(2)}) collective-permute-start(f32[88,256]{1,0:T(8,128)S(1)} %get-tuple-element.33), channel_id=1, source_target_pairs={{1,0},{2,1},{3,2},{4,3},{5,4},{6,5},{7,6},{8,7},{9,8},{10,9},{11,1... | collective-permute-start | bytes 270344 | tf_op jit(solution)/shard_map/ppermute | solution.py:22
  4.9 6.4 %collective-permute-start.1 = (f32[80,128]{1,0:T(8,128)S(1)}, f32[80,128]{1,0:T(8,128)S(1)}, u32[]{:S(2)}, u32[]{:S(2)}) collective-permute-start(f32[80,128]{1,0:T(8,128)S(1)} %get-tuple-element.30), channel_id=1, source_target_pairs={{30,0},{31,1},{0,2},{1,3},{2,4},{3,5},{4,6},{5,7},{6,8},{7,9},{8,1... | collective-permute-start | bytes 122888 | tf_op jit(solution)/shard_map/ppermute | solution.py:22
  6.1 10.2 %collective-permute-start.2 = (f32[80,128]{1,0:T(8,128)S(1)}, f32[80,128]{1,0:T(8,128)S(1)}, u32[]{:S(2)}, u32[]{:S(2)}) collective-permute-start(f32[80,128]{1,0:T(8,128)S(1)} %get-tuple-element.31), channel_id=1, source_target_pairs={{29,0},{30,1},{31,2},{0,3},{1,4},{2,5},{3,6},{4,7},{5,8},{6,9},{7,... | collective-permute-start | bytes 122888 | tf_op jit(solution)/shard_map/ppermute | solution.py:22
  8.2 9.3 %collective-permute-start.3 = (f32[80,128]{1,0:T(8,128)S(1)}, f32[80,128]{1,0:T(8,128)S(1)}, u32[]{:S(2)}, u32[]{:S(2)}) collective-permute-start(f32[80,128]{1,0:T(8,128)S(1)} %get-tuple-element.32), channel_id=1, source_target_pairs={{28,0},{29,1},{30,2},{31,3},{0,4},{1,5},{2,6},{3,7},{4,8},{5,9},{6... | collective-permute-start | bytes 122888 | tf_op jit(solution)/shard_map/ppermute | solution.py:22
  11.3 10.6 %collective-permute-start.5 = (f32[80,128]{1,0:T(8,128)S(1)}, f32[80,128]{1,0:T(8,128)S(1)}, u32[]{:S(2)}, u32[]{:S(2)}) collective-permute-start(f32[80,128]{1,0:T(8,128)S(1)} %get-tuple-element.34), channel_id=1, source_target_pairs={{2,0},{3,1},{4,2},{5,3},{6,4},{7,5},{8,6},{9,7},{10,8},{11,9},{12,... | collective-permute-start | bytes 122888 | tf_op jit(solution)/shard_map/ppermute | solution.py:22
  16.3 5.7 %collective-permute-start.6 = (f32[80,128]{1,0:T(8,128)S(1)}, f32[80,128]{1,0:T(8,128)S(1)}, u32[]{:S(2)}, u32[]{:S(2)}) collective-permute-start(f32[80,128]{1,0:T(8,128)S(1)} %get-tuple-element.35), channel_id=1, source_target_pairs={{3,0},{4,1},{5,2},{6,3},{7,4},{8,5},{9,6},{10,7},{11,8},{12,9},{13... | collective-permute-start | bytes 122888 | tf_op jit(solution)/shard_map/ppermute | solution.py:22
  17.4 4.5 %collective-permute-start.7 = (f32[80,128]{1,0:T(8,128)S(1)}, f32[80,128]{1,0:T(8,128)S(1)}, u32[]{:S(2)}, u32[]{:S(2)}) collective-permute-start(f32[80,128]{1,0:T(8,128)S(1)} %get-tuple-element.36), channel_id=1, source_target_pairs={{4,0},{5,1},{6,2},{7,3},{8,4},{9,5},{10,6},{11,7},{12,8},{13,9},{1... | collective-permute-start | bytes 122888 | tf_op jit(solution)/shard_map/ppermute | solution.py:22

commit v2 on v1

--- a/solution.py
+++ b/solution.py
@@ -88,9 +88,14 @@
 
 def read_lanes(state_hbm, lanes, sems):
     return [
-        pltpu.make_async_copy(
-            state_hbm.at[:, :, pl.ds(block * LANES, LANES)], lanes.at[block], sems.at[block]
-        )
+        [
+            pltpu.make_async_copy(
+                state_hbm.at[var, :, pl.ds(block * LANES, LANES)],
+                lanes.at[block, var],
+                sems.at[block, var],
+            )
+            for var in range(5)
+        ]
         for block in range(lanes.shape[0])
     ]
 
@@ -106,9 +111,10 @@
     return lanes[block, var, pl.ds(3 * (face % 2), 16, stride=4), :]
 
 
-def add_face(lanes, var, face, value):
-    for block in range(lanes.shape[0]):
-        part = value[:, block * LANES : (block + 1) * LANES]
+def add_face(lanes, var, face, value, begin=0):
+    for which in range(value.shape[1] // LANES):
+        block = begin + which
+        part = value[:, which * LANES : (which + 1) * LANES]
         if face < 2:
             lanes[block, var, 48 * face : 48 * face + 16, :] += part
         elif face < 4:
@@ -224,7 +230,7 @@
         for k, (source, target) in enumerate(zip(inputs[1:], targets))
     ]
     copies = read_lanes(inputs[0], lanes, state_sems)
-    for copy in loads[:4] + copies + loads[4:]:
+    for copy in loads[:4] + sum(copies, []) + loads[4:]:
         copy.start()
     slots = faces_ref.shape[1]
     count, backs = mortar_ref.shape[1], back_ref.shape[1]
@@ -277,22 +283,17 @@
         outs[target][80:88, 0:slots] = jnp.zeros((8, slots), F32)
         extra.append(trace)
 
-    for copy in copies:
-        copy.wait()
-    for face in range(6):
+    for block in range(chunks):
         for var in range(5):
-            for block in range(chunks):
+            copies[block][var].wait()
+        for var in range(5):
+            rows = slice(16 * var, 16 * var + 16)
+            for face in range(6):
                 part = face_part(lanes, block, var, face)
-                rows = slice(16 * var, 16 * var + 16)
-                columns = slice(block * LANES, (block + 1) * LANES)
-                traces[face, rows, columns] = part
+                traces[face, rows, block * LANES : (block + 1) * LANES] = part
                 if face < 4:
-                    store_pieces(
-                        pieces,
-                        16 * var,
-                        slice(face * elems + block * LANES, face * elems + (block + 1) * LANES),
-                        part,
-                    )
+                    start = face * elems + block * LANES
+                    store_pieces(pieces, 16 * var, slice(start, start + LANES), part)
 
     def collect(step, first):
         for p in range(peers):
@@ -329,7 +330,6 @@
 
 
 def local_kernel(
-    block_count,
     lanes,
     partner_ref,
     mortar_ref,
@@ -341,7 +341,6 @@
     beside_ref,
     big_ref,
     own_ref,
-    range_ref,
     pieces,
     spots,
     grid,
@@ -349,16 +348,7 @@
     elems = partner_ref.shape[1]
     chunks = elems // LANES
     count = mortar_ref.shape[1]
-    wide = 2 * LANES
     number_rows(grid)
-    links = partner_ref[...]
-    block = lax.shift_right_arithmetic(links - (6 * elems + 1), wide.bit_length() - 1)
-    least = jnp.min(jnp.where(block >= 0, block, block_count), axis=1, keepdims=True)
-    most = jnp.max(block, axis=1, keepdims=True)
-    for face in range(6):
-        range_ref[face] = jnp.minimum(least[face, 0], block_count - 1)
-        range_ref[8 + face] = most[face, 0]
-    range_ref[6] = highest(jnp.where(most > least, 1, 0))
     returned = own_ref.shape[1] // 2
     first_back = 5 * count + 1
     slot = lax.broadcasted_iota(jnp.int32, (returned, elems), 0) + first_back
@@ -469,7 +459,6 @@
         step_ref,
         spread_ref,
         gather_ref,
-        range_ref,
         out_hbm,
         sums,
         outside,
@@ -491,6 +480,11 @@
     places = packed_places(count)
 
     number_rows(grid)
+    whole_links = partner_ref[...]
+    block_of = lax.shift_right_arithmetic(whole_links - base, wide.bit_length() - 1)
+    least = jnp.min(jnp.where(block_of >= 0, block_of, peers // 2 - 1), axis=1, keepdims=True)
+    most = jnp.max(block_of, axis=1, keepdims=True)
+    starts = [least[face, 0] for face in range(6)]
     links = [partner_ref[face : face + 1, :] for face in range(6)]
     sources = [source_ref[face : face + 1, :] for face in range(4)]
 
@@ -506,8 +500,23 @@
     payload[1] = arrived[hop][:, slots:]
     codes = [payload[side, 80:81, :] for side in range(2)]
 
-    @pl.when(highest(jnp.maximum(codes[0], codes[1])) >= 0.0)
+    outside[...] = jnp.zeros(outside.shape, F32)
+    split = jnp.maximum(highest(codes[0]), highest(codes[1])) >= 0.0
+
+    @pl.when(split | (highest(most - least) > 0))
     def _():
+        for face in range(6):
+
+            @pl.loop(starts[face] + 1, most[face, 0] + 1)
+            def _(block, face=face):
+                outside[face] += joined(
+                    jnp.dot(
+                        pieces[block],
+                        one_hot(grid, links[face] - base - block * wide, wide),
+                        preferred_element_type=F32,
+                    )
+                )
+
         for side, row in ((0, hop), (1, 0)):
             code = codes[side].astype(jnp.int32)
             listed = jnp.take_along_axis(
@@ -532,32 +541,13 @@
                     0, 6 * chunks, pick, payload[side, rows, :]
                 )
 
-    @pl.when(range_ref[6] == 0)
-    def _():
-        outside[...] = jnp.zeros(outside.shape, F32)
-
-    @pl.when(range_ref[6] != 0)
-    def _():
-        for face in range(6):
-            outside[face] = jnp.zeros(outside.shape[1:], F32)
-
-            @pl.loop(range_ref[face] + 1, range_ref[8 + face] + 1)
-            def _(block, face=face):
-                outside[face] += joined(
-                    jnp.dot(
-                        pieces[block],
-                        one_hot(grid, links[face] - base - block * wide, wide),
-                        preferred_element_type=F32,
-                    )
-                )
-
     factor = (-6.0 * step_ref[0]) * jnp.left_shift(2, level_ref[...]).astype(F32)
     sums[...] = step_ref[0] * acc_ref[...]
 
     def conform(face):
         axis, sign = face // 2, 2 * (face % 2) - 1
         columns = slice(face * elems, (face + 1) * elems)
-        block = range_ref[face]
+        block = starts[face]
         near = joined(
             jnp.dot(
                 pieces[block],
@@ -674,30 +664,39 @@
     for _ in chain:
         pass
 
+    columns = []
     for face in range(4):
         entry = sources[face]
         row = sum((entry >= (k + 1) * count).astype(jnp.int32) for k in range(4))
         spot = entry - row * count
         column = jnp.where(row >= 3, LANES + (row - 3) * count, row * count) + spot
         beyond = 2 * LANES + count + entry - (5 * count + 1)
-        column = jnp.where(entry < 5 * count, column, jnp.where(entry > 5 * count, beyond, -1))
-        star = joined(
-            jnp.dot(
-                fluxes[...], one_hot(grid, column, 3 * LANES), preferred_element_type=F32
+        columns.append(
+            jnp.where(entry < 5 * count, column, jnp.where(entry > 5 * count, beyond, -1))
+        )
+    copies = []
+    span = 2 if chunks % 2 == 0 else 1
+    for begin in range(0, chunks, span):
+        part = slice(begin * LANES, (begin + span) * LANES)
+        for face in range(4):
+            star = joined(
+                jnp.dot(
+                    fluxes[...],
+                    one_hot(grid, columns[face][:, part], 3 * LANES),
+                    preferred_element_type=F32,
+                )
             )
-        )
-        for v in range(5):
-            rows = slice(16 * v, 16 * v + 16)
-            add_face(sums, v, face, factor * (stars_of[face, rows, :] + star[rows, :]))
-
-    copies = [
-        pltpu.make_async_copy(
-            sums.at[block], out_hbm.at[:, :, pl.ds(block * LANES, LANES)], sems.at[block]
-        )
-        for block in range(chunks)
-    ]
-    for copy in copies:
-        copy.start()
+            for v in range(5):
+                rows = slice(16 * v, 16 * v + 16)
+                add_face(
+                    sums, v, face, factor[:, part] * (stars_of[face, rows, part] + star[rows, :]), begin
+                )
+        for block in range(begin, begin + span):
+            copy = pltpu.make_async_copy(
+                sums.at[block], out_hbm.at[:, :, pl.ds(block * LANES, LANES)], sems.at[block]
+            )
+            copy.start()
+            copies.append(copy)
     for copy in copies:
         copy.wait()
 
@@ -748,7 +747,7 @@
             grid,
             pltpu.VMEM(return_faces.shape, jnp.int32),
             pltpu.SemaphoreType.DMA((len(inputs) - 1,)),
-            sems,
+            pltpu.SemaphoreType.DMA((chunks, 5)),
         ],
         name="send",
         compiler_params=pltpu.CompilerParams(vmem_limit_bytes=14 << 20),
@@ -760,18 +759,17 @@
     for peer in range(peers):
         distance = peer + 1 if peer < hop else hop - 1 - peer
         arrived.append(passed_along(outgoing[peer], "dev", distance))
-    acc, traces, beside, big, own, ranges = pl.pallas_call(
-        functools.partial(local_kernel, peers // 2),
+    acc, traces, beside, big, own = pl.pallas_call(
+        local_kernel,
         out_shape=[
             lanes,
             jax.ShapeDtypeStruct((80, 6 * elems), F32),
             jax.ShapeDtypeStruct((80, 6 * elems), F32),
             jax.ShapeDtypeStruct((80, 2 * LANES), F32),
             jax.ShapeDtypeStruct((80, LANES), F32),
-            jax.ShapeDtypeStruct((16,), jnp.int32),
         ],
         in_specs=[vmem] * 6,
-        out_specs=[vmem] * 5 + [smem],
+        out_specs=[vmem] * 5,
         scratch_shapes=[
             pltpu.VMEM((240, 4 * elems), BF16),
             pltpu.VMEM((8, 2 * LANES), jnp.int32),
@@ -783,7 +781,7 @@
     return pl.pallas_call(
         functools.partial(finish_kernel, base, hop, peers),
         out_shape=jax.ShapeDtypeStruct((5, 64, elems), F32),
-        in_specs=[vmem] * (peers + 11) + [smem, vmem, vmem, smem],
+        in_specs=[vmem] * (peers + 11) + [smem, vmem, vmem],
         out_specs=hbm,
         scratch_shapes=[
             pltpu.VMEM(lanes.shape, F32),
@@ -814,7 +812,6 @@
         step_size,
         spread,
         gather,
-        ranges,
     )
 
 

time: 26.1 us -> 25.5 us (0.977)
  Pallas kernels: 8.09 us -> 7.45 us
    pallas_call x1, Pallas kernels: 3.95 us -> 3.34 us  [body(): pl.pallas_call(functools.partial(finish_kernel, base, hop, peers), out_sh...]
  transfers between devices with their start and end apart: 8 -> 8, of which waited for: 2 -> 2; matrix products, arithmetic and copies ran while one was open for 0% -> 0% of each run, Pallas kernels for 7% -> 8%
where the time goes in v2:
time: 25.5 us; the launch traced here: 25.3 us
  starting transfers between devices  14.3 us (56%)
  Pallas kernels  7.45 us (29%)
  waiting for transfers between devices  2.87 us (11%)
  between operations  0.71 us (3%)
    ppermute x8, starting transfers between devices, passed_along(): return lax.ppermute(block, axis, route)  14.3 us
    pallas_call x1, Pallas kernels, body(): pl.pallas_call(functools.partial(finish_kernel, base, hop, peers), out_sh...  3.34 us
    ppermute x8, waiting for transfers between devices, passed_along(): return lax.ppermute(block, axis, route)  2.87 us
    pallas_call x1, Pallas kernels, body(): pl.pallas_call(functools.partial(send_kernel, hop, peers), out_shape=shap...  2.18 us
    pallas_call x1, Pallas kernels, body(): pl.pallas_call(local_kernel, out_shape=[lanes, jax.ShapeDtypeStruct((80,...  1.93 us
  transfers between devices with their start and end apart: 8, of which 2 were waited for; matrix products, arithmetic and copies ran while one was open for 0% of the time, Pallas kernels for 8%

profile of v2, /device:TPU:1, one launch (start us, length us, event | category | flops | bytes accessed | tf_op | source)
XLA Modules:
  0.0 25.3 jit_solution(3850493476879793578)
XLA Ops:
  0.0 2.2 %send.1 = (f32[88,256]{1,0:T(8,128)S(1)}, f32[80,128]{1,0:T(8,128)S(1)}, f32[80,128]{1,0:T(8,128)S(1)}, f32[80,128]{1,0:T(8,128)S(1)}, f32[88,256]{1,0:T(8,128)S...) custom-call(f32[5,64,512]{2,1,0:T(8,128)} %rest_0_.1, ...), custom_call_target="tpu_custom_call" | custom-call | tf_op jit(solution)/shard_map/send/pallas_call | solution.py:737
  2.2 2.6 %collective-permute-start = (f32[88,256]{1,0:T(8,128)S(1)}, f32[88,256]{1,0:T(8,128)S(1)}, u32[]{:S(2)}, u32[]{:S(2)}) collective-permute-start(f32[88,256]{1,0:T(8,128)S(1)} %get-tuple-element.28), channel_id=1, source_target_pairs={{31,0},{0,1},{1,2},{2,3},{3,4},{4,5},{5,6},{6,7},{7,8},{8,9},{9,10... | collective-permute-start | bytes 270344 | tf_op jit(solution)/shard_map/ppermute | solution.py:22
  4.8 0.0 collective-permute-start.4
  4.8 1.2 %collective-permute-start.1 = (f32[80,128]{1,0:T(8,128)S(1)}, f32[80,128]{1,0:T(8,128)S(1)}, u32[]{:S(2)}, u32[]{:S(2)}) collective-permute-start(f32[80,128]{1,0:T(8,128)S(1)} %get-tuple-element.29), channel_id=1, source_target_pairs={{30,0},{31,1},{0,2},{1,3},{2,4},{3,5},{4,6},{5,7},{6,8},{7,9},{8,1... | collective-permute-start | bytes 122888 | tf_op jit(solution)/shard_map/ppermute | solution.py:22
  6.0 2.1 %collective-permute-start.2 = (f32[80,128]{1,0:T(8,128)S(1)}, f32[80,128]{1,0:T(8,128)S(1)}, u32[]{:S(2)}, u32[]{:S(2)}) collective-permute-start(f32[80,128]{1,0:T(8,128)S(1)} %get-tuple-element.30), channel_id=1, source_target_pairs={{29,0},{30,1},{31,2},{0,3},{1,4},{2,5},{3,6},{4,7},{5,8},{6,9},{7,... | collective-permute-start | bytes 122888 | tf_op jit(solution)/shard_map/ppermute | solution.py:22
  8.1 1.6 %collective-permute-start.3 = (f32[80,128]{1,0:T(8,128)S(1)}, f32[80,128]{1,0:T(8,128)S(1)}, u32[]{:S(2)}, u32[]{:S(2)}) collective-permute-start(f32[80,128]{1,0:T(8,128)S(1)} %get-tuple-element.31), channel_id=1, source_target_pairs={{28,0},{29,1},{30,2},{31,3},{0,4},{1,5},{2,6},{3,7},{4,8},{5,9},{6... | collective-permute-start | bytes 122888 | tf_op jit(solution)/shard_map/ppermute | solution.py:22
  9.6 1.6 %collective-permute-done.1.rest_1_ = f32[80,128]{1,0:T(8,128)S(1)} collective-permute-done((f32[80,128]{1,0:T(8,128)S(1)}, f32[80,128]{1,0:T(8,128)S(1)}, u32[]{:S(2)}, u32[]{:S(2)}) %collective-permute-start.1) | collective-permute-done | bytes 40992 | tf_op jit(solution)/shard_map/ppermute | solution.py:22
  11.3 3.7 %collective-permute-start.5 = (f32[80,128]{1,0:T(8,128)S(1)}, f32[80,128]{1,0:T(8,128)S(1)}, u32[]{:S(2)}, u32[]{:S(2)}) collective-permute-start(f32[80,128]{1,0:T(8,128)S(1)} %get-tuple-element.33), channel_id=1, source_target_pairs={{2,0},{3,1},{4,2},{5,3},{6,4},{7,5},{8,6},{9,7},{10,8},{11,9},{12,... | collective-permute-start | bytes 122888 | tf_op jit(solution)/shard_map/ppermute | solution.py:22
  15.0 1.2 %collective-permute-done.2.rest_2_ = f32[80,128]{1,0:T(8,128)S(1)} collective-permute-done((f32[80,128]{1,0:T(8,128)S(1)}, f32[80,128]{1,0:T(8,128)S(1)}, u32[]{:S(2)}, u32[]{:S(2)}) %collective-permute-start.2) | collective-permute-done | bytes 40992 | tf_op jit(solution)/shard_map/ppermute | solution.py:22
  16.2 1.2 %collective-permute-start.6 = (f32[80,128]{1,0:T(8,128)S(1)}, f32[80,128]{1,0:T(8,128)S(1)}, u32[]{:S(2)}, u32[]{:S(2)}) collective-permute-start(f32[80,128]{1,0:T(8,128)S(1)} %get-tuple-element.34), channel_id=1, source_target_pairs={{3,0},{4,1},{5,2},{6,3},{7,4},{8,5},{9,6},{10,7},{11,8},{12,9},{13... | collective-permute-start | bytes 122888 | tf_op jit(solution)/shard_map/ppermute | solution.py:22
  17.4 0.0 collective-permute-done.3.rest_3_
  17.4 1.9 %collective-permute-start.7 = (f32[80,128]{1,0:T(8,128)S(1)}, f32[80,128]{1,0:T(8,128)S(1)}, u32[]{:S(2)}, u32[]{:S(2)}) collective-permute-start(f32[80,128]{1,0:T(8,128)S(1)} %get-tuple-element.35), channel_id=1, source_target_pairs={{4,0},{5,1},{6,2},{7,3},{8,4},{9,5},{10,6},{11,7},{12,8},{13,9},{1... | collective-permute-start | bytes 122888 | tf_op jit(solution)/shard_map/ppermute | solution.py:22
  20.0 1.9 %local.1 = (f32[4,5,64,128]{3,2,1,0:T(8,128)S(1)}, f32[80,3072]{1,0:T(8,128)S(1)}, f32[80,3072]{1,0:T(8,128)S(1)}, f32[80,256]{1,0:T(8,128)S(1)}, f32[80,128]{1,0:T(8,128)S(1)}) custom-call(f32[4,5,64,128]{3,2,1,0:T(8,128)S(1)} %get-tuple-element.36.lanes, s32[6,512]{1,0:T(8,128)S(1)} %get-tuple-element.37.partner_ref.rest_13_, ...), custom_call_target="tpu_custom_call" | custom-call | tf_op jit(solution)/shard_map/local/pallas_call | solution.py:762
  21.9 0.0 collective-permute-done.5.rest_5_
  21.9 0.0 collective-permute-done.6.rest_6_
  21.9 0.0 collective-permute-done.7.rest_7_
  21.9 0.0 collective-permute-done.rest_0_
  22.0 0.0 collective-permute-done.4.rest_4_
  22.0 3.3 %finish.1 = f32[5,64,512]{2,1,0:T(8,128)} custom-call(f32[88,256]{1,0:T(8,128)S(1)} %collective-permute-done.rest_0_, f32[80,128]{1,0:T(8,128)S(1)} %collective-permute-done.1.rest_1_, f32[80,128]{1,0:T(8,128)S(1)} %collective-permute-done.2.rest_2_, f32[80,128]{1,0:T(8,128)S(1)} %collective-permute-done.3.rest_3_, ...), custom_call_target="tpu_custom_call" | custom-call | tf_op jit(solution)/shard_map/finish/pallas_call | solution.py:781
Async XLA Ops:
  2.2 19.8 %collective-permute-start = (f32[88,256]{1,0:T(8,128)S(1)}, f32[88,256]{1,0:T(8,128)S(1)}, u32[]{:S(2)}, u32[]{:S(2)}) collective-permute-start(f32[88,256]{1,0:T(8,128)S(1)} %get-tuple-element.28), channel_id=1, source_target_pairs={{31,0},{0,1},{1,2},{2,3},{3,4},{4,5},{5,6},{6,7},{7,8},{8,9},{9,10... | collective-permute-start | bytes 270344 | tf_op jit(solution)/shard_map/ppermute | solution.py:22
  4.8 17.1 %collective-permute-start.4 = (f32[88,256]{1,0:T(8,128)S(1)}, f32[88,256]{1,0:T(8,128)S(1)}, u32[]{:S(2)}, u32[]{:S(2)}) collective-permute-start(f32[88,256]{1,0:T(8,128)S(1)} %get-tuple-element.32), channel_id=1, source_target_pairs={{1,0},{2,1},{3,2},{4,3},{5,4},{6,5},{7,6},{8,7},{9,8},{10,9},{11,1... | collective-permute-start | bytes 270344 | tf_op jit(solution)/shard_map/ppermute | solution.py:22
  4.8 6.4 %collective-permute-start.1 = (f32[80,128]{1,0:T(8,128)S(1)}, f32[80,128]{1,0:T(8,128)S(1)}, u32[]{:S(2)}, u32[]{:S(2)}) collective-permute-start(f32[80,128]{1,0:T(8,128)S(1)} %get-tuple-element.29), channel_id=1, source_target_pairs={{30,0},{31,1},{0,2},{1,3},{2,4},{3,5},{4,6},{5,7},{6,8},{7,9},{8,1... | collective-permute-start | bytes 122888 | tf_op jit(solution)/shard_map/ppermute | solution.py:22
  6.0 10.2 %collective-permute-start.2 = (f32[80,128]{1,0:T(8,128)S(1)}, f32[80,128]{1,0:T(8,128)S(1)}, u32[]{:S(2)}, u32[]{:S(2)}) collective-permute-start(f32[80,128]{1,0:T(8,128)S(1)} %get-tuple-element.30), channel_id=1, source_target_pairs={{29,0},{30,1},{31,2},{0,3},{1,4},{2,5},{3,6},{4,7},{5,8},{6,9},{7,... | collective-permute-start | bytes 122888 | tf_op jit(solution)/shard_map/ppermute | solution.py:22
  8.1 9.3 %collective-permute-start.3 = (f32[80,128]{1,0:T(8,128)S(1)}, f32[80,128]{1,0:T(8,128)S(1)}, u32[]{:S(2)}, u32[]{:S(2)}) collective-permute-start(f32[80,128]{1,0:T(8,128)S(1)} %get-tuple-element.31), channel_id=1, source_target_pairs={{28,0},{29,1},{30,2},{31,3},{0,4},{1,5},{2,6},{3,7},{4,8},{5,9},{6... | collective-permute-start | bytes 122888 | tf_op jit(solution)/shard_map/ppermute | solution.py:22
  11.3 10.6 %collective-permute-start.5 = (f32[80,128]{1,0:T(8,128)S(1)}, f32[80,128]{1,0:T(8,128)S(1)}, u32[]{:S(2)}, u32[]{:S(2)}) collective-permute-start(f32[80,128]{1,0:T(8,128)S(1)} %get-tuple-element.33), channel_id=1, source_target_pairs={{2,0},{3,1},{4,2},{5,3},{6,4},{7,5},{8,6},{9,7},{10,8},{11,9},{12,... | collective-permute-start | bytes 122888 | tf_op jit(solution)/shard_map/ppermute | solution.py:22
  16.2 5.7 %collective-permute-start.6 = (f32[80,128]{1,0:T(8,128)S(1)}, f32[80,128]{1,0:T(8,128)S(1)}, u32[]{:S(2)}, u32[]{:S(2)}) collective-permute-start(f32[80,128]{1,0:T(8,128)S(1)} %get-tuple-element.34), channel_id=1, source_target_pairs={{3,0},{4,1},{5,2},{6,3},{7,4},{8,5},{9,6},{10,7},{11,8},{12,9},{13... | collective-permute-start | bytes 122888 | tf_op jit(solution)/shard_map/ppermute | solution.py:22
  17.4 4.6 %collective-permute-start.7 = (f32[80,128]{1,0:T(8,128)S(1)}, f32[80,128]{1,0:T(8,128)S(1)}, u32[]{:S(2)}, u32[]{:S(2)}) collective-permute-start(f32[80,128]{1,0:T(8,128)S(1)} %get-tuple-element.35), channel_id=1, source_target_pairs={{4,0},{5,1},{6,2},{7,3},{8,4},{9,5},{10,6},{11,7},{12,8},{13,9},{1... | collective-permute-start | bytes 122888 | tf_op jit(solution)/shard_map/ppermute | solution.py:22
